TPU v7x, 32 devices: a whole 2x2x4 slice. The times are simulated.
32 devices in a mesh: grp: 2 (over x), chan: 16 (over z, y, core).
Axes of the slice: x: 2, y: 2, z: 4, core: 2. Of those that a mesh axis runs over, the one named last changes fastest.
Arguments:
- voltages: bfloat16 [2048, 38912], P(('grp', 'chan')), parts along dimension 0, may hold values from -6 to 6
- steering_delays: bfloat16 [512, 1024], replicated, may hold values from 0 to 1
- trial_delays: int32 [256, 512], replicated, may hold values from 0 to 7
- beam_order: int32 [512], replicated, may hold values from 0 to 511, each once
Outputs:
- trial_power: float32 [2, 1024, 4, 256], P(None, ('grp', 'chan')), parts along dimension 1
There are 2 independent parts, one for each index of `grp`. A program takes and returns all parts, laid end to end along the dimension named above; an argument that names none is the same for every part. Nothing has to cross between parts.
Inputs may be any that keep to these rules, and one draw needn't show every extreme that they name: `beam_order`: each beam appears exactly once.
All inputs are finite; a program needn't handle non-finite values.
Results may differ from a plain program's by a relative error of at most 0.0094.
Values may be sent and summed in bfloat16 or wider, within the bound.
A program may use at most 64 MiB of HBM per device.

v0:
```python
import math

import jax
import jax.numpy as jnp
from jax import lax
from jax.sharding import PartitionSpec as P

TRANSFORM_SIZE = 2048
CHANNELS = 512
POLYPHASE_TAPS = 4
ANTENNAS = 1024
BEAM_COUNT = 512
BLOCK_FRAMES = 8
BLOCK_COUNT = 2
CHANNELS_PER_SET = 4
FLUCT_BINS = 4
ALL_FRAMES = 16


TWO_PI = 2.0 * math.pi


def prototype():
    length = POLYPHASE_TAPS * TRANSFORM_SIZE
    position = jnp.arange(length, dtype=jnp.float32)
    centred = (position - 0.5 * (length - 1)) / TRANSFORM_SIZE
    hamming = 0.54 - 0.46 * jnp.cos(TWO_PI * position / (length - 1))
    shaped = jnp.sinc(centred) * hamming
    return (shaped / jnp.sqrt(jnp.sum(shaped * shaped))).reshape(POLYPHASE_TAPS, TRANSFORM_SIZE)


def fluctuation_table():
    frame_index = jnp.arange(BLOCK_FRAMES, dtype=jnp.int32)
    bin_index = jnp.arange(1, FLUCT_BINS + 1, dtype=jnp.int32)
    phase_turns = frame_index[:, None] * bin_index[None, :] % BLOCK_FRAMES
    phase_angle = phase_turns.astype(jnp.float32) * (TWO_PI / BLOCK_FRAMES)
    return jnp.concatenate([jnp.cos(phase_angle), -jnp.sin(phase_angle)], 1).astype(jnp.bfloat16)


def trial_tables(trial_delays):
    bin_index = jnp.arange(1, FLUCT_BINS + 1, dtype=jnp.int32)
    phase_turns = bin_index[:, None, None] * trial_delays[None, :, :] % BLOCK_FRAMES
    phase_angle = phase_turns.astype(jnp.float32) * (TWO_PI / BLOCK_FRAMES)
    return (jnp.cos(phase_angle).astype(jnp.bfloat16), jnp.sin(phase_angle).astype(jnp.bfloat16))


def shards(voltages, steering_delays, trial_delays, beam_order):
    device_list = lax.axis_size("chan")
    device = lax.axis_index("chan")
    antenna_local = voltages.shape[0]
    chan_local = CHANNELS // device_list
    channel_set_count = chan_local // CHANNELS_PER_SET
    window = prototype()
    voltage_block_list = voltages.reshape(
        antenna_local, ALL_FRAMES + POLYPHASE_TAPS - 1, TRANSFORM_SIZE
    )
    window_applied = voltage_block_list[:, 0:ALL_FRAMES, :] * window[0]
    for tap_index in range(1, POLYPHASE_TAPS):
        window_applied = (
            window_applied
            + voltage_block_list[:, tap_index : tap_index + ALL_FRAMES, :] * window[tap_index]
        )
    frame_rows = window_applied.astype(jnp.bfloat16).reshape(
        antenna_local * ALL_FRAMES, TRANSFORM_SIZE
    )
    slot_index = jnp.arange(CHANNELS_PER_SET, dtype=jnp.int32)
    owner_index = jnp.arange(device_list, dtype=jnp.int32)
    group_ids = jnp.arange(channel_set_count, dtype=jnp.int32)
    channel_ids = (
        owner_index[None, :, None] * chan_local
        + group_ids[:, None, None] * CHANNELS_PER_SET
        + slot_index[None, None, :]
    )
    sample = jnp.arange(TRANSFORM_SIZE, dtype=jnp.int32)
    phase_turns = (
        channel_ids.reshape(channel_set_count, 1, device_list * CHANNELS_PER_SET, 1)
        * sample
        % TRANSFORM_SIZE
    )
    phase_angle = phase_turns.astype(jnp.float32) * (TWO_PI / TRANSFORM_SIZE)
    filter_rows = jnp.concatenate([jnp.cos(phase_angle), -jnp.sin(phase_angle)], 1).astype(
        jnp.bfloat16
    )
    filter_rows = filter_rows.reshape(2 * CHANNELS, TRANSFORM_SIZE)
    spectra = lax.dot_general(
        filter_rows, frame_rows, (((1,), (1,)), ((), ())), preferred_element_type=jnp.float32
    )
    spectra = spectra.astype(jnp.bfloat16).reshape(
        channel_set_count, 2, device_list * CHANNELS_PER_SET, antenna_local * ALL_FRAMES
    )
    steering = steering_delays[beam_order].astype(jnp.float32)
    time_table = fluctuation_table()

    def beam_group(block_data, group_index):
        real_input = block_data[0].reshape(CHANNELS_PER_SET, ANTENNAS, ALL_FRAMES)
        imaginary_input = block_data[1].reshape(CHANNELS_PER_SET, ANTENNAS, ALL_FRAMES)
        channel_values = (device * chan_local + group_index * CHANNELS_PER_SET + slot_index).astype(
            jnp.float32
        )
        factor = TWO_PI * (1.0 + channel_values / CHANNELS)
        phases = steering[None, :, :] * factor[:, None, None]
        cosine_weights = jnp.cos(phases).astype(jnp.bfloat16)
        sine_weights = jnp.sin(phases).astype(jnp.bfloat16)
        beam_real = jnp.einsum(
            "gat,gba->gtb", real_input, cosine_weights, preferred_element_type=jnp.float32
        ) + jnp.einsum(
            "gat,gba->gtb", imaginary_input, sine_weights, preferred_element_type=jnp.float32
        )
        beam_imag = jnp.einsum(
            "gat,gba->gtb", imaginary_input, cosine_weights, preferred_element_type=jnp.float32
        ) - jnp.einsum("gat,gba->gtb", real_input, sine_weights, preferred_element_type=jnp.float32)
        intensity = (beam_real * beam_real + beam_imag * beam_imag).astype(jnp.bfloat16)
        intensity = intensity.reshape(CHANNELS_PER_SET, BLOCK_COUNT, BLOCK_FRAMES, BEAM_COUNT)
        return jnp.einsum(
            "gnfb,fj->bnjg", intensity, time_table, preferred_element_type=jnp.float32
        ).astype(jnp.bfloat16)

    blank_buffer = jnp.zeros((BEAM_COUNT, BLOCK_COUNT, 2 * FLUCT_BINS, chan_local), jnp.bfloat16)
    turned = lax.all_to_all(spectra, "chan", split_axis=2, concat_axis=3, tiled=True)

    def step_whole(group_index, buffer):
        block_data = lax.dynamic_index_in_dim(turned, group_index, 0, keepdims=False)
        result = beam_group(block_data, group_index)
        return lax.dynamic_update_slice_in_dim(buffer, result, group_index * CHANNELS_PER_SET, 3)

    gathered = lax.fori_loop(0, channel_set_count, step_whole, blank_buffer)
    trial_cos, trial_sin = trial_tables(trial_delays)
    normaliser = 1.0 / (CHANNELS * BLOCK_FRAMES * ANTENNAS * ANTENNAS)
    exchanged = lax.all_to_all(gathered, "chan", split_axis=0, concat_axis=3, tiled=True)
    real_part = exchanged[:, :, :FLUCT_BINS, :]
    imag_part = exchanged[:, :, FLUCT_BINS:, :]
    sum_real = jnp.einsum(
        "bnkc,kdc->nbkd", real_part, trial_cos, preferred_element_type=jnp.float32
    ) - jnp.einsum("bnkc,kdc->nbkd", imag_part, trial_sin, preferred_element_type=jnp.float32)
    sum_imag = jnp.einsum(
        "bnkc,kdc->nbkd", real_part, trial_sin, preferred_element_type=jnp.float32
    ) + jnp.einsum("bnkc,kdc->nbkd", imag_part, trial_cos, preferred_element_type=jnp.float32)
    return (sum_real * sum_real + sum_imag * sum_imag) * normaliser


def solution(mesh):
    return jax.shard_map(
        shards,
        mesh=mesh,
        in_specs=(P(("grp", "chan"), None), P(), P(), P()),
        out_specs=P(None, ("grp", "chan"), None, None),
        check_vma=False,
    )
```

profile of v0, /device:TPU:0, one launch (start us, length us, event | category | flops | bytes accessed | tf_op | source)
XLA Modules:
  0.0 1122.0 jit_solution(15527053644622948887)
XLA Ops:
  1.7 8.4 reshape.190
  10.4 18.1 %cosine_convert_fusion = (bf16[8,1,64,2048]{3,2,1,0:T(8,128)(2,1)S(1)}, bf16[8,1,64,2048]{3,2,1,0:T(8,128)(2,1)S(1)}) fusion(s32[8,64]{1,0:T(8,128)S(1)} %copy.30), kind=kLoop, calls=%fused_computation.45 | loop fusion | flops 17825792 | bytes 4196352 | tf_op jit(solution)/shard_map/convert.2
  30.1 4.3 add_convert_fusion
  34.3 4.8 convolution_convert_fusion.1
  39.1 3.5 copy.31
  42.6 7.8 all-to-all-start
  56.2 35.2 %all-to-all-done = bf16[8,2,64,1024]{3,1,0,2:T(2,128)(2,1)S(1)} async-done(((bf16[8,2,64,1024]{3,1,0,2:T(2,128)(2,1)}), bf16[8,2,64,1024]{3,1,0,2:T(2,128)(2,1)S(1)}, u32[]{:S(2)}, u32[]{:S(2)}) %all-to-all-start) | async-done | bytes 2097184 | tf_op jit(solution)/shard_map/all_to_all | solution.py:119
  93.9 4.5 all_to_all.29
  99.2 948.5 %while.16 = (s32[]{:T(128)}, bf16[512,2,8,32]{0,2,1,3:T(8,128)(2,1)}, bf16[8,2,4,16384]{3,2,1,0:T(4,128)(2,1)}, f32[512,1024]{1,0:T(8,128)}, s32[]{:T(128)}, /*i...) while((s32[]{:T(128)}, ...), condition=%wide.region_2.3_spmd.clone, body=%wide.region_1.2_spmd.clone.sunk | while | flops 285966368 | bytes 19202480 | solution.py:126
  101.6 28.9 %fusion.154 = f32[4,16,512]{2,1,0:T(8,128)S(1)} fusion(bf16[4,1024,16]{2,1,0:T(8,128)(2,1)S(1)} %squeeze.26, f32[4]{0:T(128)S(1)} %fusion.153, f32[512,1024]{1,0:T(8,128)} %get-tuple-element.278), kind=kOutput, calls=%fused_computation.6.clone.1 | convolution fusion | flops 71303168 | bytes 2359312 | tf_op jit(solution)/shard_map/while/body/eval_jaxpr/gat,gba->gtb/dot_general | solution.py:111
  131.3 28.6 %fusion.155 = f32[4,16,512]{2,1,0:T(8,128)S(1)} fusion(f32[4,16,512]{2,1,0:T(8,128)S(1)} %fusion.154, bf16[4,1024,16]{2,1,0:T(8,128)(2,1)S(1)} %squeeze.27, f32[4]{0:T(128)S(1)} %fusion.153, f32[512,1024]{1,0:T(8,128)} %get-tuple-element.278), kind=kOutput, calls=%fused_computation.22.clone.1 | convolution fusion | flops 71368704 | bytes 2490384 | tf_op jit(solution)/shard_map/while/body/eval_jaxpr/gat,gba->gtb/dot_general | solution.py:109
  159.9 28.1 %fusion.156 = f32[4,16,512]{2,1,0:T(8,128)S(1)} fusion(bf16[4,1024,16]{2,1,0:T(8,128)(2,1)S(1)} %squeeze.27, f32[4]{0:T(128)S(1)} %fusion.153, f32[512,1024]{1,0:T(8,128)S(1)} %copy-done.1), kind=kOutput, calls=%fused_computation.7.clone.1 | convolution fusion | flops 71303168 | bytes 2359312 | tf_op jit(solution)/shard_map/while/body/eval_jaxpr/gat,gba->gtb/dot_general | solution.py:106
  188.0 29.3 %fusion.157 = bf16[512,2,8,32]{0,2,1,3:T(8,128)(2,1)} fusion(bf16[512,2,8,32]{0,2,1,3:T(8,128)(2,1)} %get-tuple-element.265, s32[]{:T(128)S(6)} %select_n.223, f32[4,16,512]{2,1,0:T(8,128)S(1)} %fusion.155, f32[4,16,512]{2,1,0:T(8,128)S(1)} %fusion.156, bf16[4,1024,16]{2,1,0:T(8,128)(2,1)S(1)} %squeeze.26, f32[4]{0:T(128)S(1)} %fusion.153, ...), kind=kOutput, calls=%fused_computation.26.clone.1 | convolution fusion | flops 71991296 | bytes 2556052 | tf_op jit(solution)/shard_map/while/body/eval_jaxpr/gnfb,fj->bnjg/dot_general | solution.py:114
  219.5 28.9 %fusion.154 = f32[4,16,512]{2,1,0:T(8,128)S(1)} fusion(bf16[4,1024,16]{2,1,0:T(8,128)(2,1)S(1)} %squeeze.26, f32[4]{0:T(128)S(1)} %fusion.153, f32[512,1024]{1,0:T(8,128)} %get-tuple-element.278), kind=kOutput, calls=%fused_computation.6.clone.1 | convolution fusion | flops 71303168 | bytes 2359312 | tf_op jit(solution)/shard_map/while/body/eval_jaxpr/gat,gba->gtb/dot_general | solution.py:111
  249.2 28.6 %fusion.155 = f32[4,16,512]{2,1,0:T(8,128)S(1)} fusion(f32[4,16,512]{2,1,0:T(8,128)S(1)} %fusion.154, bf16[4,1024,16]{2,1,0:T(8,128)(2,1)S(1)} %squeeze.27, f32[4]{0:T(128)S(1)} %fusion.153, f32[512,1024]{1,0:T(8,128)} %get-tuple-element.278), kind=kOutput, calls=%fused_computation.22.clone.1 | convolution fusion | flops 71368704 | bytes 2490384 | tf_op jit(solution)/shard_map/while/body/eval_jaxpr/gat,gba->gtb/dot_general | solution.py:109
  277.8 28.1 %fusion.156 = f32[4,16,512]{2,1,0:T(8,128)S(1)} fusion(bf16[4,1024,16]{2,1,0:T(8,128)(2,1)S(1)} %squeeze.27, f32[4]{0:T(128)S(1)} %fusion.153, f32[512,1024]{1,0:T(8,128)S(1)} %copy-done.1), kind=kOutput, calls=%fused_computation.7.clone.1 | convolution fusion | flops 71303168 | bytes 2359312 | tf_op jit(solution)/shard_map/while/body/eval_jaxpr/gat,gba->gtb/dot_general | solution.py:106
  305.9 29.3 %fusion.157 = bf16[512,2,8,32]{0,2,1,3:T(8,128)(2,1)} fusion(bf16[512,2,8,32]{0,2,1,3:T(8,128)(2,1)} %get-tuple-element.265, s32[]{:T(128)S(6)} %select_n.223, f32[4,16,512]{2,1,0:T(8,128)S(1)} %fusion.155, f32[4,16,512]{2,1,0:T(8,128)S(1)} %fusion.156, bf16[4,1024,16]{2,1,0:T(8,128)(2,1)S(1)} %squeeze.26, f32[4]{0:T(128)S(1)} %fusion.153, ...), kind=kOutput, calls=%fused_computation.26.clone.1 | convolution fusion | flops 71991296 | bytes 2556052 | tf_op jit(solution)/shard_map/while/body/eval_jaxpr/gnfb,fj->bnjg/dot_general | solution.py:114
  337.4 28.9 %fusion.154 = f32[4,16,512]{2,1,0:T(8,128)S(1)} fusion(bf16[4,1024,16]{2,1,0:T(8,128)(2,1)S(1)} %squeeze.26, f32[4]{0:T(128)S(1)} %fusion.153, f32[512,1024]{1,0:T(8,128)} %get-tuple-element.278), kind=kOutput, calls=%fused_computation.6.clone.1 | convolution fusion | flops 71303168 | bytes 2359312 | tf_op jit(solution)/shard_map/while/body/eval_jaxpr/gat,gba->gtb/dot_general | solution.py:111
  367.1 28.6 %fusion.155 = f32[4,16,512]{2,1,0:T(8,128)S(1)} fusion(f32[4,16,512]{2,1,0:T(8,128)S(1)} %fusion.154, bf16[4,1024,16]{2,1,0:T(8,128)(2,1)S(1)} %squeeze.27, f32[4]{0:T(128)S(1)} %fusion.153, f32[512,1024]{1,0:T(8,128)} %get-tuple-element.278), kind=kOutput, calls=%fused_computation.22.clone.1 | convolution fusion | flops 71368704 | bytes 2490384 | tf_op jit(solution)/shard_map/while/body/eval_jaxpr/gat,gba->gtb/dot_general | solution.py:109
  395.7 28.1 %fusion.156 = f32[4,16,512]{2,1,0:T(8,128)S(1)} fusion(bf16[4,1024,16]{2,1,0:T(8,128)(2,1)S(1)} %squeeze.27, f32[4]{0:T(128)S(1)} %fusion.153, f32[512,1024]{1,0:T(8,128)S(1)} %copy-done.1), kind=kOutput, calls=%fused_computation.7.clone.1 | convolution fusion | flops 71303168 | bytes 2359312 | tf_op jit(solution)/shard_map/while/body/eval_jaxpr/gat,gba->gtb/dot_general | solution.py:106
  423.8 29.3 %fusion.157 = bf16[512,2,8,32]{0,2,1,3:T(8,128)(2,1)} fusion(bf16[512,2,8,32]{0,2,1,3:T(8,128)(2,1)} %get-tuple-element.265, s32[]{:T(128)S(6)} %select_n.223, f32[4,16,512]{2,1,0:T(8,128)S(1)} %fusion.155, f32[4,16,512]{2,1,0:T(8,128)S(1)} %fusion.156, bf16[4,1024,16]{2,1,0:T(8,128)(2,1)S(1)} %squeeze.26, f32[4]{0:T(128)S(1)} %fusion.153, ...), kind=kOutput, calls=%fused_computation.26.clone.1 | convolution fusion | flops 71991296 | bytes 2556052 | tf_op jit(solution)/shard_map/while/body/eval_jaxpr/gnfb,fj->bnjg/dot_general | solution.py:114
  455.3 28.9 %fusion.154 = f32[4,16,512]{2,1,0:T(8,128)S(1)} fusion(bf16[4,1024,16]{2,1,0:T(8,128)(2,1)S(1)} %squeeze.26, f32[4]{0:T(128)S(1)} %fusion.153, f32[512,1024]{1,0:T(8,128)} %get-tuple-element.278), kind=kOutput, calls=%fused_computation.6.clone.1 | convolution fusion | flops 71303168 | bytes 2359312 | tf_op jit(solution)/shard_map/while/body/eval_jaxpr/gat,gba->gtb/dot_general | solution.py:111
  485.0 28.6 %fusion.155 = f32[4,16,512]{2,1,0:T(8,128)S(1)} fusion(f32[4,16,512]{2,1,0:T(8,128)S(1)} %fusion.154, bf16[4,1024,16]{2,1,0:T(8,128)(2,1)S(1)} %squeeze.27, f32[4]{0:T(128)S(1)} %fusion.153, f32[512,1024]{1,0:T(8,128)} %get-tuple-element.278), kind=kOutput, calls=%fused_computation.22.clone.1 | convolution fusion | flops 71368704 | bytes 2490384 | tf_op jit(solution)/shard_map/while/body/eval_jaxpr/gat,gba->gtb/dot_general | solution.py:109
  513.6 28.1 %fusion.156 = f32[4,16,512]{2,1,0:T(8,128)S(1)} fusion(bf16[4,1024,16]{2,1,0:T(8,128)(2,1)S(1)} %squeeze.27, f32[4]{0:T(128)S(1)} %fusion.153, f32[512,1024]{1,0:T(8,128)S(1)} %copy-done.1), kind=kOutput, calls=%fused_computation.7.clone.1 | convolution fusion | flops 71303168 | bytes 2359312 | tf_op jit(solution)/shard_map/while/body/eval_jaxpr/gat,gba->gtb/dot_general | solution.py:106
  541.7 29.3 %fusion.157 = bf16[512,2,8,32]{0,2,1,3:T(8,128)(2,1)} fusion(bf16[512,2,8,32]{0,2,1,3:T(8,128)(2,1)} %get-tuple-element.265, s32[]{:T(128)S(6)} %select_n.223, f32[4,16,512]{2,1,0:T(8,128)S(1)} %fusion.155, f32[4,16,512]{2,1,0:T(8,128)S(1)} %fusion.156, bf16[4,1024,16]{2,1,0:T(8,128)(2,1)S(1)} %squeeze.26, f32[4]{0:T(128)S(1)} %fusion.153, ...), kind=kOutput, calls=%fused_computation.26.clone.1 | convolution fusion | flops 71991296 | bytes 2556052 | tf_op jit(solution)/shard_map/while/body/eval_jaxpr/gnfb,fj->bnjg/dot_general | solution.py:114
  573.2 28.9 %fusion.154 = f32[4,16,512]{2,1,0:T(8,128)S(1)} fusion(bf16[4,1024,16]{2,1,0:T(8,128)(2,1)S(1)} %squeeze.26, f32[4]{0:T(128)S(1)} %fusion.153, f32[512,1024]{1,0:T(8,128)} %get-tuple-element.278), kind=kOutput, calls=%fused_computation.6.clone.1 | convolution fusion | flops 71303168 | bytes 2359312 | tf_op jit(solution)/shard_map/while/body/eval_jaxpr/gat,gba->gtb/dot_general | solution.py:111
  602.9 28.6 %fusion.155 = f32[4,16,512]{2,1,0:T(8,128)S(1)} fusion(f32[4,16,512]{2,1,0:T(8,128)S(1)} %fusion.154, bf16[4,1024,16]{2,1,0:T(8,128)(2,1)S(1)} %squeeze.27, f32[4]{0:T(128)S(1)} %fusion.153, f32[512,1024]{1,0:T(8,128)} %get-tuple-element.278), kind=kOutput, calls=%fused_computation.22.clone.1 | convolution fusion | flops 71368704 | bytes 2490384 | tf_op jit(solution)/shard_map/while/body/eval_jaxpr/gat,gba->gtb/dot_general | solution.py:109
  631.5 28.1 %fusion.156 = f32[4,16,512]{2,1,0:T(8,128)S(1)} fusion(bf16[4,1024,16]{2,1,0:T(8,128)(2,1)S(1)} %squeeze.27, f32[4]{0:T(128)S(1)} %fusion.153, f32[512,1024]{1,0:T(8,128)S(1)} %copy-done.1), kind=kOutput, calls=%fused_computation.7.clone.1 | convolution fusion | flops 71303168 | bytes 2359312 | tf_op jit(solution)/shard_map/while/body/eval_jaxpr/gat,gba->gtb/dot_general | solution.py:106
  659.6 29.3 %fusion.157 = bf16[512,2,8,32]{0,2,1,3:T(8,128)(2,1)} fusion(bf16[512,2,8,32]{0,2,1,3:T(8,128)(2,1)} %get-tuple-element.265, s32[]{:T(128)S(6)} %select_n.223, f32[4,16,512]{2,1,0:T(8,128)S(1)} %fusion.155, f32[4,16,512]{2,1,0:T(8,128)S(1)} %fusion.156, bf16[4,1024,16]{2,1,0:T(8,128)(2,1)S(1)} %squeeze.26, f32[4]{0:T(128)S(1)} %fusion.153, ...), kind=kOutput, calls=%fused_computation.26.clone.1 | convolution fusion | flops 71991296 | bytes 2556052 | tf_op jit(solution)/shard_map/while/body/eval_jaxpr/gnfb,fj->bnjg/dot_general | solution.py:114
  691.2 28.9 %fusion.154 = f32[4,16,512]{2,1,0:T(8,128)S(1)} fusion(bf16[4,1024,16]{2,1,0:T(8,128)(2,1)S(1)} %squeeze.26, f32[4]{0:T(128)S(1)} %fusion.153, f32[512,1024]{1,0:T(8,128)} %get-tuple-element.278), kind=kOutput, calls=%fused_computation.6.clone.1 | convolution fusion | flops 71303168 | bytes 2359312 | tf_op jit(solution)/shard_map/while/body/eval_jaxpr/gat,gba->gtb/dot_general | solution.py:111
  720.8 28.6 %fusion.155 = f32[4,16,512]{2,1,0:T(8,128)S(1)} fusion(f32[4,16,512]{2,1,0:T(8,128)S(1)} %fusion.154, bf16[4,1024,16]{2,1,0:T(8,128)(2,1)S(1)} %squeeze.27, f32[4]{0:T(128)S(1)} %fusion.153, f32[512,1024]{1,0:T(8,128)} %get-tuple-element.278), kind=kOutput, calls=%fused_computation.22.clone.1 | convolution fusion | flops 71368704 | bytes 2490384 | tf_op jit(solution)/shard_map/while/body/eval_jaxpr/gat,gba->gtb/dot_general | solution.py:109
  749.4 28.1 %fusion.156 = f32[4,16,512]{2,1,0:T(8,128)S(1)} fusion(bf16[4,1024,16]{2,1,0:T(8,128)(2,1)S(1)} %squeeze.27, f32[4]{0:T(128)S(1)} %fusion.153, f32[512,1024]{1,0:T(8,128)S(1)} %copy-done.1), kind=kOutput, calls=%fused_computation.7.clone.1 | convolution fusion | flops 71303168 | bytes 2359312 | tf_op jit(solution)/shard_map/while/body/eval_jaxpr/gat,gba->gtb/dot_general | solution.py:106
  777.5 29.3 %fusion.157 = bf16[512,2,8,32]{0,2,1,3:T(8,128)(2,1)} fusion(bf16[512,2,8,32]{0,2,1,3:T(8,128)(2,1)} %get-tuple-element.265, s32[]{:T(128)S(6)} %select_n.223, f32[4,16,512]{2,1,0:T(8,128)S(1)} %fusion.155, f32[4,16,512]{2,1,0:T(8,128)S(1)} %fusion.156, bf16[4,1024,16]{2,1,0:T(8,128)(2,1)S(1)} %squeeze.26, f32[4]{0:T(128)S(1)} %fusion.153, ...), kind=kOutput, calls=%fused_computation.26.clone.1 | convolution fusion | flops 71991296 | bytes 2556052 | tf_op jit(solution)/shard_map/while/body/eval_jaxpr/gnfb,fj->bnjg/dot_general | solution.py:114
  809.1 28.9 %fusion.154 = f32[4,16,512]{2,1,0:T(8,128)S(1)} fusion(bf16[4,1024,16]{2,1,0:T(8,128)(2,1)S(1)} %squeeze.26, f32[4]{0:T(128)S(1)} %fusion.153, f32[512,1024]{1,0:T(8,128)} %get-tuple-element.278), kind=kOutput, calls=%fused_computation.6.clone.1 | convolution fusion | flops 71303168 | bytes 2359312 | tf_op jit(solution)/shard_map/while/body/eval_jaxpr/gat,gba->gtb/dot_general | solution.py:111
  838.7 28.6 %fusion.155 = f32[4,16,512]{2,1,0:T(8,128)S(1)} fusion(f32[4,16,512]{2,1,0:T(8,128)S(1)} %fusion.154, bf16[4,1024,16]{2,1,0:T(8,128)(2,1)S(1)} %squeeze.27, f32[4]{0:T(128)S(1)} %fusion.153, f32[512,1024]{1,0:T(8,128)} %get-tuple-element.278), kind=kOutput, calls=%fused_computation.22.clone.1 | convolution fusion | flops 71368704 | bytes 2490384 | tf_op jit(solution)/shard_map/while/body/eval_jaxpr/gat,gba->gtb/dot_general | solution.py:109
  867.4 28.1 %fusion.156 = f32[4,16,512]{2,1,0:T(8,128)S(1)} fusion(bf16[4,1024,16]{2,1,0:T(8,128)(2,1)S(1)} %squeeze.27, f32[4]{0:T(128)S(1)} %fusion.153, f32[512,1024]{1,0:T(8,128)S(1)} %copy-done.1), kind=kOutput, calls=%fused_computation.7.clone.1 | convolution fusion | flops 71303168 | bytes 2359312 | tf_op jit(solution)/shard_map/while/body/eval_jaxpr/gat,gba->gtb/dot_general | solution.py:106
  895.4 29.3 %fusion.157 = bf16[512,2,8,32]{0,2,1,3:T(8,128)(2,1)} fusion(bf16[512,2,8,32]{0,2,1,3:T(8,128)(2,1)} %get-tuple-element.265, s32[]{:T(128)S(6)} %select_n.223, f32[4,16,512]{2,1,0:T(8,128)S(1)} %fusion.155, f32[4,16,512]{2,1,0:T(8,128)S(1)} %fusion.156, bf16[4,1024,16]{2,1,0:T(8,128)(2,1)S(1)} %squeeze.26, f32[4]{0:T(128)S(1)} %fusion.153, ...), kind=kOutput, calls=%fused_computation.26.clone.1 | convolution fusion | flops 71991296 | bytes 2556052 | tf_op jit(solution)/shard_map/while/body/eval_jaxpr/gnfb,fj->bnjg/dot_general | solution.py:114
  927.0 28.9 %fusion.154 = f32[4,16,512]{2,1,0:T(8,128)S(1)} fusion(bf16[4,1024,16]{2,1,0:T(8,128)(2,1)S(1)} %squeeze.26, f32[4]{0:T(128)S(1)} %fusion.153, f32[512,1024]{1,0:T(8,128)} %get-tuple-element.278), kind=kOutput, calls=%fused_computation.6.clone.1 | convolution fusion | flops 71303168 | bytes 2359312 | tf_op jit(solution)/shard_map/while/body/eval_jaxpr/gat,gba->gtb/dot_general | solution.py:111
  956.6 28.6 %fusion.155 = f32[4,16,512]{2,1,0:T(8,128)S(1)} fusion(f32[4,16,512]{2,1,0:T(8,128)S(1)} %fusion.154, bf16[4,1024,16]{2,1,0:T(8,128)(2,1)S(1)} %squeeze.27, f32[4]{0:T(128)S(1)} %fusion.153, f32[512,1024]{1,0:T(8,128)} %get-tuple-element.278), kind=kOutput, calls=%fused_computation.22.clone.1 | convolution fusion | flops 71368704 | bytes 2490384 | tf_op jit(solution)/shard_map/while/body/eval_jaxpr/gat,gba->gtb/dot_general | solution.py:109
  985.3 28.1 %fusion.156 = f32[4,16,512]{2,1,0:T(8,128)S(1)} fusion(bf16[4,1024,16]{2,1,0:T(8,128)(2,1)S(1)} %squeeze.27, f32[4]{0:T(128)S(1)} %fusion.153, f32[512,1024]{1,0:T(8,128)S(1)} %copy-done.1), kind=kOutput, calls=%fused_computation.7.clone.1 | convolution fusion | flops 71303168 | bytes 2359312 | tf_op jit(solution)/shard_map/while/body/eval_jaxpr/gat,gba->gtb/dot_general | solution.py:106
  1013.3 29.3 %fusion.157 = bf16[512,2,8,32]{0,2,1,3:T(8,128)(2,1)} fusion(bf16[512,2,8,32]{0,2,1,3:T(8,128)(2,1)} %get-tuple-element.265, s32[]{:T(128)S(6)} %select_n.223, f32[4,16,512]{2,1,0:T(8,128)S(1)} %fusion.155, f32[4,16,512]{2,1,0:T(8,128)S(1)} %fusion.156, bf16[4,1024,16]{2,1,0:T(8,128)(2,1)S(1)} %squeeze.26, f32[4]{0:T(128)S(1)} %fusion.153, ...), kind=kOutput, calls=%fused_computation.26.clone.1 | convolution fusion | flops 71991296 | bytes 2556052 | tf_op jit(solution)/shard_map/while/body/eval_jaxpr/gnfb,fj->bnjg/dot_general | solution.py:114
  1047.7 3.8 copy.33
  1054.2 25.6 %all_to_all.36 = bf16[16,2,8192]{2,1,0:T(2,128)(2,1)} all-to-all(bf16[16,2,8192]{2,1,0:T(2,128)(2,1)} %reshape.206), channel_id=1, replica_groups=mesh['grp'=2,'chan'=16] {'chan'}, dimensions={0} | all-to-all | bytes 1048576 | tf_op jit(solution)/shard_map/all_to_all | solution.py:129
  1085.5 3.6 all_to_all.33
  1089.2 7.7 fusion.70
  1096.9 8.2 fusion.66
  1105.1 8.0 fusion.63
  1113.1 7.8 fusion.62
  (84 shorter events, 41.9 us)
Async XLA Ops:
  0.0 50.5 %copy-start = (bf16[512,1024]{1,0:T(8,128)(2,1)S(1)}, bf16[512,1024]{1,0:T(8,128)(2,1)}, u32[]{:S(2)}) copy-start(bf16[512,1024]{1,0:T(8,128)(2,1)} %param.7) | copy-start | bytes 3145732
  10.4 18.5 %slice-start = ((s8[6291456]{0:T(1024)(128)(4,1)}), s8[4194304]{0:T(1024)(128)(4,1)S(1)}, s32[]{:S(2)}) async-start(s8[6291456]{0:T(1024)(128)(4,1)} %bitcast.64), calls=%async_computation.2 | async-start | bytes 8388608
  28.5 1.6 slice-start.1
  42.6 7.9 copy-start.2
  42.6 48.8 %all-to-all-start = ((bf16[8,2,64,1024]{3,1,0,2:T(2,128)(2,1)}), bf16[8,2,64,1024]{3,1,0,2:T(2,128)(2,1)S(1)}, u32[]{:S(2)}, u32[]{:S(2)}) async-start(bf16[8,2,64,1024]{3,1,0,2:T(2,128)(2,1)} %copy.31), calls=%async_computation | async-start | bytes 4194304 | tf_op jit(solution)/shard_map/all_to_all | solution.py:119
  131.2 28.6 %copy-start.1 = (f32[512,1024]{1,0:T(8,128)S(1)}, f32[512,1024]{1,0:T(8,128)}, u32[]{:S(2)}) copy-start(f32[512,1024]{1,0:T(8,128)} %get-tuple-element.278) | copy-start | bytes 6291460 | tf_op jit(solution)/shard_map/while
  249.2 28.6 %copy-start.1 = (f32[512,1024]{1,0:T(8,128)S(1)}, f32[512,1024]{1,0:T(8,128)}, u32[]{:S(2)}) copy-start(f32[512,1024]{1,0:T(8,128)} %get-tuple-element.278) | copy-start | bytes 6291460 | tf_op jit(solution)/shard_map/while
  367.1 28.6 %copy-start.1 = (f32[512,1024]{1,0:T(8,128)S(1)}, f32[512,1024]{1,0:T(8,128)}, u32[]{:S(2)}) copy-start(f32[512,1024]{1,0:T(8,128)} %get-tuple-element.278) | copy-start | bytes 6291460 | tf_op jit(solution)/shard_map/while
  485.0 28.6 %copy-start.1 = (f32[512,1024]{1,0:T(8,128)S(1)}, f32[512,1024]{1,0:T(8,128)}, u32[]{:S(2)}) copy-start(f32[512,1024]{1,0:T(8,128)} %get-tuple-element.278) | copy-start | bytes 6291460 | tf_op jit(solution)/shard_map/while
  602.9 28.6 %copy-start.1 = (f32[512,1024]{1,0:T(8,128)S(1)}, f32[512,1024]{1,0:T(8,128)}, u32[]{:S(2)}) copy-start(f32[512,1024]{1,0:T(8,128)} %get-tuple-element.278) | copy-start | bytes 6291460 | tf_op jit(solution)/shard_map/while
  720.8 28.6 %copy-start.1 = (f32[512,1024]{1,0:T(8,128)S(1)}, f32[512,1024]{1,0:T(8,128)}, u32[]{:S(2)}) copy-start(f32[512,1024]{1,0:T(8,128)} %get-tuple-element.278) | copy-start | bytes 6291460 | tf_op jit(solution)/shard_map/while
  838.7 28.6 %copy-start.1 = (f32[512,1024]{1,0:T(8,128)S(1)}, f32[512,1024]{1,0:T(8,128)}, u32[]{:S(2)}) copy-start(f32[512,1024]{1,0:T(8,128)} %get-tuple-element.278) | copy-start | bytes 6291460 | tf_op jit(solution)/shard_map/while
  956.6 28.6 %copy-start.1 = (f32[512,1024]{1,0:T(8,128)S(1)}, f32[512,1024]{1,0:T(8,128)}, u32[]{:S(2)}) copy-start(f32[512,1024]{1,0:T(8,128)} %get-tuple-element.278) | copy-start | bytes 6291460 | tf_op jit(solution)/shard_map/while
  1085.5 3.6 copy-start.3
where the time goes:
time: 1130 us; the launch traced here: 1120 us
  matrix products  955 us (85%)
  local copies, waits for them, and re-layouts  61.2 us (5%)
  waiting for transfers between devices  35.2 us (3%)
  other arithmetic  26.9 us (2%)
  blocking collectives  25.6 us (2%)
    dot_general x8, matrix products, beam_group(): jnp.einsum('gnfb,fj->bnjg', intensity, time_table, preferred_element_type...  235 us
    dot_general x8, matrix products, beam_group(): jnp.einsum('gat,gba->gtb', real_input, sine_weights, preferred_element_ty...  231 us
    dot_general x8, matrix products, beam_group(): jnp.einsum('gat,gba->gtb', imaginary_input, cosine_weights, preferred_ele...  229 us
    dot_general x8, matrix products, beam_group(): jnp.einsum('gat,gba->gtb', imaginary_input, sine_weights, preferred_eleme...  224 us
    all_to_all x1, waiting for transfers between devices, shards(): lax.all_to_all(spectra, 'chan', split_axis=2, concat_axis=3, tiled=True)  35.2 us
    all_to_all x1, blocking collectives, shards(): lax.all_to_all(gathered, 'chan', split_axis=0, concat_axis=3, tiled=True)  25.6 us
  transfers between devices with their start and end apart: 1, of which 1 were waited for; matrix products, arithmetic and copies ran while one was open for 1% of the time, Pallas kernels for 0%

commit v1 on v0

v1 whole, which is shorter than its diff:
```python
import functools
import math

import jax
import jax.numpy as jnp
from jax import lax
from jax.experimental import pallas as pl
from jax.experimental.pallas import tpu as pltpu
from jax.sharding import PartitionSpec as P

TRANSFORM_SIZE = 2048
POLYPHASE_TAPS = 4
BLOCK_FRAMES = 8
FLUCT_BINS = 4

TWO_PI = 2.0 * math.pi
HALF_ROOT = math.sqrt(0.5)
ROWS = 16
COLS = 256


def prototype():
    length = POLYPHASE_TAPS * TRANSFORM_SIZE
    position = jnp.arange(length, dtype=jnp.float32)
    centred = (position - 0.5 * (length - 1)) / TRANSFORM_SIZE
    hamming = 0.54 - 0.46 * jnp.cos(TWO_PI * position / (length - 1))
    shaped = jnp.sinc(centred) * hamming
    return (shaped / jnp.sqrt(jnp.sum(shaped * shaped))).reshape(POLYPHASE_TAPS, TRANSFORM_SIZE)


def time_table(blocks):
    frame_index = jnp.arange(BLOCK_FRAMES, dtype=jnp.int32)
    bin_index = jnp.arange(1, FLUCT_BINS + 1, dtype=jnp.int32)
    turns = bin_index[:, None] * frame_index[None, :] % BLOCK_FRAMES
    angle = turns.astype(jnp.float32) * (TWO_PI / BLOCK_FRAMES)
    one = jnp.concatenate([jnp.cos(angle), -jnp.sin(angle)], 0)
    return jnp.kron(jnp.eye(blocks, dtype=jnp.float32), one).astype(jnp.bfloat16)


def eighth_cos(turns):
    folded = jnp.where(turns > 4, 8 - turns, turns)
    upper = jnp.where(folded == 0, 1.0, jnp.where(folded == 1, HALF_ROOT, 0.0))
    lower = jnp.where(folded == 4, -1.0, jnp.where(folded == 3, -HALF_ROOT, 0.0))
    return upper + lower


def trial_tables(trial_delays):
    bin_index = jnp.arange(1, FLUCT_BINS + 1, dtype=jnp.int32)
    turns = (bin_index[:, None, None] * trial_delays[None, :, :]) & (BLOCK_FRAMES - 1)
    cosine = eighth_cos(turns).astype(jnp.bfloat16)
    sine = eighth_cos((turns + 6) & (BLOCK_FRAMES - 1)).astype(jnp.bfloat16)
    return cosine, sine


def polynomial(x, coefficients):
    total = coefficients[-1]
    for value in coefficients[-2::-1]:
        total = total * x + value
    return total


COS_TERMS = [(-1.0) ** i / math.factorial(2 * i) for i in range(7)]
SIN_TERMS = [(-1.0) ** i / math.factorial(2 * i + 1) for i in range(7)]


def cos_sin_turns(turns):
    reduced = turns - jnp.floor(turns + 0.5)
    half = reduced * math.pi
    square = half * half
    cosine = polynomial(square, COS_TERMS)
    sine = half * polynomial(square, SIN_TERMS)
    return 1.0 - 2.0 * sine * sine, 2.0 * sine * cosine


def beam_kernel(channels, first_ref, steer_ref, x_ref, table_ref, out_ref, weights):
    group = x_ref.shape[0]
    frames = x_ref.shape[1] // 2
    antennas, beams = steer_ref.shape
    first = first_ref[0] + pl.program_id(0) * group
    factor = 1.0 + first.astype(jnp.float32) * (1.0 / channels)

    def rows_step(index, carry):
        rows = pl.ds(pl.multiple_of(index * ROWS, ROWS), ROWS)
        for start in range(0, beams, COLS):
            cols = pl.ds(start, COLS)
            delay = steer_ref[rows, cols].astype(jnp.float32)
            cosine, sine = cos_sin_turns(delay * factor)
            step = delay * (TWO_PI / channels)
            square = step * step
            step_cos = polynomial(square, COS_TERMS[:4])
            step_sin = step * polynomial(square, SIN_TERMS[:4])
            double = step_cos + step_cos
            cos_before = cosine * step_cos + sine * step_sin
            sin_before = sine * step_cos - cosine * step_sin
            for slot in range(group):
                weights[slot, 0, rows, cols] = cosine.astype(jnp.bfloat16)
                weights[slot, 1, rows, cols] = sine.astype(jnp.bfloat16)
                if slot + 1 < group:
                    cosine, cos_before = double * cosine - cos_before, cosine
                    sine, sin_before = double * sine - sin_before, sine
        return carry

    lax.fori_loop(0, antennas // ROWS, rows_step, 0)

    def channel_step(slot, carry):
        x = x_ref[slot]
        by_cos = jnp.dot(x, weights[slot, 0], preferred_element_type=jnp.float32)
        by_sin = jnp.dot(x, weights[slot, 1], preferred_element_type=jnp.float32)
        real = by_cos[:frames] + by_sin[frames:]
        imag = by_cos[frames:] - by_sin[:frames]
        intensity = (real * real + imag * imag).astype(jnp.bfloat16)
        out_ref[slot] = jnp.dot(
            table_ref[...], intensity, preferred_element_type=jnp.float32
        ).astype(jnp.bfloat16)
        return carry

    lax.fori_loop(0, group, channel_step, 0)


def form_beams(first, steering, spectra, table, channels):
    chan_local, double_frames, antennas = spectra.shape
    beams = steering.shape[1]
    group = math.gcd(chan_local, 8)
    rows = table.shape[0]
    return pl.pallas_call(
        functools.partial(beam_kernel, channels),
        grid=(chan_local // group,),
        out_shape=jax.ShapeDtypeStruct((chan_local, rows, beams), jnp.bfloat16),
        in_specs=[
            pl.BlockSpec(memory_space=pltpu.SMEM),
            pl.BlockSpec((antennas, beams), lambda i: (0, 0)),
            pl.BlockSpec((group, double_frames, antennas), lambda i: (i, 0, 0)),
            pl.BlockSpec(table.shape, lambda i: (0, 0)),
        ],
        out_specs=pl.BlockSpec((group, rows, beams), lambda i: (i, 0, 0)),
        scratch_shapes=[pltpu.VMEM((group, 2, antennas, beams), jnp.bfloat16)],
        compiler_params=pltpu.CompilerParams(vmem_limit_bytes=40 * 1024 * 1024),
    )(first, steering, spectra, table)


def shards(voltages, steering_delays, trial_delays, beam_order):
    devices = lax.axis_size("chan")
    device = lax.axis_index("chan")
    antenna_local, samples = voltages.shape
    beams, antennas = steering_delays.shape
    trials, channels = trial_delays.shape
    all_frames = samples // TRANSFORM_SIZE - POLYPHASE_TAPS + 1
    blocks = all_frames // BLOCK_FRAMES
    chan_local = channels // devices
    beam_local = beams // devices

    window = prototype()
    pieces = [
        voltages[:, i * TRANSFORM_SIZE : (i + 1) * TRANSFORM_SIZE]
        for i in range(all_frames + POLYPHASE_TAPS - 1)
    ]
    stacked = jnp.stack(pieces, 0)
    frames = stacked[:all_frames] * window[0]
    for tap in range(1, POLYPHASE_TAPS):
        frames = frames + stacked[tap : tap + all_frames] * window[tap]
    frame_rows = frames.astype(jnp.bfloat16).reshape(all_frames * antenna_local, TRANSFORM_SIZE)

    channel_ids = jnp.arange(channels, dtype=jnp.int32)
    sample = jnp.arange(TRANSFORM_SIZE, dtype=jnp.int32)
    turns = channel_ids[:, None] * sample[None, :] & (TRANSFORM_SIZE - 1)
    phase_turns = turns.astype(jnp.float32) * (1.0 / TRANSFORM_SIZE)
    cosine, sine = cos_sin_turns(phase_turns)
    filter_rows = jnp.stack([cosine.astype(jnp.bfloat16), (-sine).astype(jnp.bfloat16)], 0)
    filter_rows = filter_rows.reshape(2 * channels, TRANSFORM_SIZE)
    spectra = lax.dot_general(
        filter_rows, frame_rows, (((1,), (1,)), ((), ())), preferred_element_type=jnp.float32
    ).astype(jnp.bfloat16)
    spectra = spectra.reshape(2, devices, chan_local, all_frames * antenna_local)
    turned = lax.all_to_all(spectra, "chan", split_axis=1, concat_axis=1, tiled=True)
    turned = turned.reshape(2, devices, chan_local, all_frames, antenna_local)
    turned = turned.transpose(2, 0, 3, 1, 4).reshape(chan_local, 2 * all_frames, antennas)

    steering = steering_delays[beam_order].T
    first = (device * chan_local).astype(jnp.int32).reshape(1)
    fluctuation = form_beams(first, steering, turned, time_table(blocks), channels)

    outgoing = fluctuation.reshape(chan_local, 2 * FLUCT_BINS * blocks, devices, beam_local)
    outgoing = outgoing.transpose(2, 1, 3, 0)
    exchanged = lax.all_to_all(outgoing, "chan", split_axis=0, concat_axis=0, tiled=True)
    exchanged = exchanged.reshape(devices, blocks, 2, FLUCT_BINS, beam_local, chan_local)
    parts = exchanged.transpose(3, 1, 4, 2, 0, 5).reshape(
        FLUCT_BINS, blocks * beam_local, 2 * channels
    )
    trial_cos, trial_sin = trial_tables(trial_delays)
    both = jnp.concatenate(
        [
            jnp.concatenate([trial_cos, -trial_sin], 2),
            jnp.concatenate([trial_sin, trial_cos], 2),
        ],
        1,
    )
    sums = lax.dot_general(
        parts, both, (((2,), (2,)), ((0,), (0,))), preferred_element_type=jnp.float32
    )
    normaliser = 1.0 / (channels * BLOCK_FRAMES * antennas * antennas)
    sum_real, sum_imag = sums[..., :trials], sums[..., trials:]
    power = (sum_real * sum_real + sum_imag * sum_imag) * normaliser
    return power.reshape(FLUCT_BINS, blocks, beam_local, trials).transpose(1, 2, 0, 3)


def solution(mesh):
    return jax.shard_map(
        shards,
        mesh=mesh,
        in_specs=(P(("grp", "chan"), None), P(), P(), P()),
        out_specs=P(None, ("grp", "chan"), None, None),
        check_vma=False,
    )
```

time: 1130 us -> 217 us (0.19)
  matrix products: 955 us -> 7.91 us
  Pallas kernels: 0 us -> 46 us
  blocking collectives: 25.6 us -> 0 us
  waiting for transfers between devices: 35.2 us -> 46.7 us
    dot_general x36 -> x1, matrix products: 951 us -> 3.14 us  [shards(): lax.dot_general(parts, both, (((2,), (2,)), ((0,), (0,))), preferred_elem...]
    pallas_call x0 -> x1, Pallas kernels: none -> 46 us  [form_beams(): pl.pallas_call(functools.partial(beam_kernel, channels), grid=(chan_local...]
    all_to_all x1 -> x0, blocking collectives: 25.6 us -> none  [shards(): lax.all_to_all(gathered, 'chan', split_axis=0, concat_axis=3, tiled=True)]
    unnamed x12 -> x73, local copies, waits for them, and re-layouts: 6.92 us -> 29.3 us
    another operation x2 -> x1, other arithmetic: 18.2 us -> 2.13 us  [shards(): jnp.stack([cosine.astype(jnp.bfloat16), (-sine).astype(jnp.bfloat16)], 0)]
    convert_element_type x2 -> x6, other arithmetic: 7.08 us -> 19.9 us  [the longest x1 6.57 us: shards(): frames.astype(jnp.bfloat16)]
    squeeze x16 -> x0, local copies, waits for them, and re-layouts: 12.1 us -> none  [the longest x8 6.05 us: beam_group(): real_input = block_data[0].reshape(CHANNELS_PER_SET, ANTENNAS, ALL_FRAMES)]
    reshape x2 -> x8, local copies, waits for them, and re-layouts: 11.9 us -> 23.6 us  [the longest x1 5.47 us: shards(): turned.transpose(2, 0, 3, 1, 4)]
  transfers between devices with their start and end apart: 1 -> 2, of which waited for: 1 -> 2; matrix products, arithmetic and copies ran while one was open for 1% -> 4% of each run, Pallas kernels for 0% -> 0%
where the time goes in v1:
time: 217 us; the launch traced here: 216 us
  local copies, waits for them, and re-layouts  70.1 us (32%)
  waiting for transfers between devices  46.7 us (22%)
  Pallas kernels  46 us (21%)
  other arithmetic  25.4 us (12%)
  starting transfers between devices  18.7 us (9%)
  matrix products  7.91 us (4%)
    pallas_call x1, Pallas kernels, form_beams(): pl.pallas_call(functools.partial(beam_kernel, channels), grid=(chan_local...  46 us
    all_to_all x1, waiting for transfers between devices, shards(): lax.all_to_all(spectra, 'chan', split_axis=1, concat_axis=1, tiled=True)  38 us
    unnamed x73, local copies, waits for them, and re-layouts  29.3 us
    all_to_all x1, starting transfers between devices, shards(): lax.all_to_all(outgoing, 'chan', split_axis=0, concat_axis=0, tiled=True)  11.2 us
    transpose x1, local copies, waits for them, and re-layouts, shards(): turned.transpose(2, 0, 3, 1, 4)  9.03 us
    all_to_all x1, waiting for transfers between devices, shards(): lax.all_to_all(outgoing, 'chan', split_axis=0, concat_axis=0, tiled=True)  8.69 us
    all_to_all x1, starting transfers between devices, shards(): lax.all_to_all(spectra, 'chan', split_axis=1, concat_axis=1, tiled=True)  7.48 us
    convert_element_type x1, other arithmetic, shards(): frames.astype(jnp.bfloat16)  6.57 us
  transfers between devices with their start and end apart: 2, of which 2 were waited for; matrix products, arithmetic and copies ran while one was open for 4% of the time, Pallas kernels for 0%

profile of v1, /device:TPU:0, one launch (start us, length us, event | category | flops | bytes accessed | tf_op | source)
XLA Modules:
  0.0 215.9 jit_solution(11574637910322879876)
XLA Ops:
  0.0 0.8 multiply_reduce_fusion
  0.8 3.6 %fusion.1 = bf16[1,512,2048]{2,1,0:T(8,128)(2,1)S(1)} fusion(), kind=kLoop, calls=%fused_computation.7 | loop fusion | flops 27262976 | bytes 2097152 | tf_op jit(solution)/shard_map/convert_element_type | solution.py:168
  4.4 6.3 %fusion.3 = bf16[1,512,2048]{2,1,0:T(8,128)(2,1)} fusion(), kind=kLoop, calls=%fused_computation.9 | loop fusion | flops 39845888 | bytes 2097152 | tf_op jit(solution)/shard_map/convert_element_type | solution.py:168
  10.7 1.0 bitcast_dynamic-update-slice_fusion.63
  11.7 1.0 bitcast_dynamic-update-slice_fusion.62
  13.0 0.8 bitcast_dynamic-update-slice_fusion.13
  13.8 0.9 bitcast_dynamic-update-slice_fusion.9
  15.1 1.2 bitcast_dynamic-update-slice_fusion.5
  16.3 0.8 bitcast_dynamic-update-slice_fusion.47
  17.0 1.2 bitcast_dynamic-update-slice_fusion.43
  19.6 0.7 bitcast_dynamic-update-slice_fusion.31
  20.4 0.7 bitcast_dynamic-update-slice_fusion.27
  21.1 0.7 bitcast_dynamic-update-slice_fusion.23
  21.8 0.7 bitcast_dynamic-update-slice_fusion.19
  22.5 0.7 bitcast_dynamic-update-slice_fusion.15
  24.7 0.7 bitcast_dynamic-update-slice_fusion.4
  25.4 0.8 bitcast_dynamic-update-slice_fusion.2
  27.7 0.7 bitcast_dynamic-update-slice_fusion.34
  29.1 0.7 bitcast_dynamic-update-slice_fusion.26
  30.6 0.7 bitcast_dynamic-update-slice_fusion.18
  32.7 0.7 bitcast_dynamic-update-slice_fusion.6
  34.9 0.7 bitcast_dynamic-update-slice_fusion
  36.5 2.1 pad_maximum_fusion
  39.3 1.3 copy-done.7
  40.6 6.6 %add_convert_fusion = bf16[16,64,2048]{2,1,0:T(8,128)(2,1)S(1)} fusion(bf16[16,64,2048]{2,1,0:T(8,128)(2,1)} %bitcast_dynamic-update-slice_fusion, bf16[16,64,2048]{2,1,0:T(8,128)(2,1)} %get-tuple-element.17, bf16[16,64,2048]{2,1,0:T(8,128)(2,1)S(1)} %copy-done.5, bf16[16,64,2048]{2,1,0:T(8,128)(2,1)S(1)} %copy-done.7, f32[2048]{0:T(1024)S(1)} %get-tuple-element.22, ...), kind=kLoop, calls=%fused_computation.1 | loop fusion | flops 25165824 | bytes 21004288 | tf_op jit(solution)/shard_map/convert_element_type | solution.py:161
  47.2 4.8 %convolution_convert_fusion = bf16[1024,1024]{1,0:T(8,128)(2,1)S(1)} fusion(bf16[1024,2048]{1,0:T(8,128)(2,1)S(1)} %bitcast.119, bf16[1024,2048]{1,0:T(8,128)(2,1)S(1)} %bitcast.118), kind=kOutput, calls=%fused_computation.41 | convolution fusion | flops 4296015872 | bytes 10485760 | tf_op jit(solution)/shard_map/dot_general | solution.py:170
  51.9 1.5 copy.13
  53.4 7.5 %all-to-all-start = ((bf16[2,16,32,1024]{3,2,0,1:T(8,128)(2,1)}), bf16[2,16,32,1024]{3,2,0,1:T(8,128)(2,1)}, u32[]{:S(2)}, u32[]{:S(2)}) async-start(bf16[2,16,32,1024]{3,2,0,1:T(8,128)(2,1)} %copy.13), calls=%async_computation | async-start | bytes 4194304 | tf_op jit(solution)/shard_map/all_to_all | solution.py:174
  61.3 2.1 gather_fusion
  63.9 38.0 %all-to-all-done = bf16[2,16,32,1024]{3,2,0,1:T(8,128)(2,1)} async-done(((bf16[2,16,32,1024]{3,2,0,1:T(8,128)(2,1)}), bf16[2,16,32,1024]{3,2,0,1:T(8,128)(2,1)}, u32[]{:S(2)}, u32[]{:S(2)}) %all-to-all-start) | async-done | bytes 2097184 | tf_op jit(solution)/shard_map/all_to_all | solution.py:174
  101.9 1.8 copy.14
  103.7 4.0 %reshape.274 = bf16[2,16,32,16,64]{4,3,2,1,0:T(8,128)(2,1)} reshape(bf16[2,16,32,1024]{3,2,1,0:T(8,128)(2,1)S(1)} %copy.14) | data formatting | bytes 4194304 | tf_op jit(solution)/shard_map/reshape | solution.py:175
  107.7 9.0 %copy.15 = bf16[32,2,16,16,64]{4,3,2,1,0:T(8,128)(2,1)} copy(bf16[32,2,16,16,64]{4,2,0,3,1:T(8,128)(2,1)} %bitcast.114) | data formatting | bytes 4194304 | tf_op jit(solution)/shard_map/transpose | solution.py:176
  116.8 5.5 %reshape.275.x_ref = bf16[32,32,1024]{2,1,0:T(8,128)(2,1)S(1)} reshape(bf16[32,2,16,16,64]{4,3,2,1,0:T(8,128)(2,1)} %copy.15) | data formatting | bytes 4194304 | tf_op jit(solution)/shard_map/reshape | solution.py:176
  122.2 46.0 %shard_map.46 = bf16[32,16,512]{2,1,0:T(8,128)(2,1)S(1)} custom-call(s32[1]{0:T(128)} %bitcast.first_ref, bf16[1024,512]{1,0:T(8,128)(2,1)S(1)} %bitcast.113, bf16[32,32,1024]{2,1,0:T(8,128)(2,1)S(1)} %reshape.275.x_ref, bf16[16,16]{1,0:T(8,128)(2,1)S(1)} %convert_element_type.127.table_ref), custom_call_target="tpu_custom_call" | custom-call | tf_op jit(solution)/shard_map/pallas_call | solution.py:125
  168.2 0.8 copy-done.2
  169.0 2.7 %reshape.276 = bf16[32,16,16,32]{3,2,1,0:T(8,128)(2,1)S(1)} reshape(bf16[32,16,512]{2,1,0:T(8,128)(2,1)} %copy-done.2) | data formatting | bytes 1048576 | tf_op jit(solution)/shard_map/reshape | solution.py:182
  171.7 1.9 copy.24
  173.6 4.5 %reshape.289 = bf16[16,2,8192]{2,1,0:T(2,128)(2,1)} reshape(bf16[16,32,16,32]{3,2,1,0:T(8,128)(2,1)} %bitcast.115) | data formatting | bytes 1048576
  178.1 11.2 %all-to-all-start.1 = ((bf16[16,2,8192]{2,1,0:T(2,128)(2,1)}), bf16[16,2,8192]{2,1,0:T(2,128)(2,1)S(1)}, u32[]{:S(2)}, u32[]{:S(2)}) async-start(bf16[16,2,8192]{2,1,0:T(2,128)(2,1)} %reshape.289), calls=%async_computation.1 | async-start | bytes 1048576 | tf_op jit(solution)/shard_map/all_to_all | solution.py:184
  189.4 2.2 %fusion.59 = bf16[4,256,512]{2,1,0:T(8,128)(2,1)} fusion(s32[256,512]{1,0:T(8,128)S(1)} %copy-done.8, s32[4]{0:T(128)S(1)} %iota_add_fusion.1), kind=kLoop, calls=%fused_computation.164 | loop fusion | flops 10485760 | bytes 1572880 | tf_op jit(solution)/shard_map/neg | solution.py:192
  191.6 3.3 %add_convert_fusion.1 = (bf16[4,256,512]{2,1,0:T(8,128)(2,1)}, bf16[4,256,512]{2,1,0:T(8,128)(2,1)}) fusion(s32[256,512]{1,0:T(8,128)S(1)} %copy-done.8, s32[4]{0:T(128)S(1)} %iota_add_fusion.1), kind=kLoop, calls=%fused_computation.30 | loop fusion | flops 15728640 | bytes 2621456 | tf_op jit(solution)/shard_map/convert_element_type | solution.py:51
  195.0 8.7 %all-to-all-done.1 = bf16[16,2,8192]{2,1,0:T(2,128)(2,1)S(1)} async-done(((bf16[16,2,8192]{2,1,0:T(2,128)(2,1)}), bf16[16,2,8192]{2,1,0:T(2,128)(2,1)S(1)}, u32[]{:S(2)}, u32[]{:S(2)}) %all-to-all-start.1) | async-done | bytes 524320 | tf_op jit(solution)/shard_map/all_to_all | solution.py:184
  203.6 1.0 reshape.290
  204.7 3.6 %copy.17 = bf16[16,2,2,4,32,32]{5,0,2,4,1,3:T(8,128)(2,1)} copy(bf16[16,2,2,4,32,32]{4,3,2,1,5,0:T(4,128)(2,1)S(1)} %bitcast.116) | data formatting | bytes 1048576 | tf_op jit(solution)/shard_map/reshape | solution.py:185
  208.3 3.5 %reshape.278 = bf16[4,64,1024]{2,1,0:T(8,128)(2,1)S(1)} reshape(bf16[4,2,32,2,16,32]{5,4,3,2,1,0:T(8,128)(2,1)} %bitcast.117) | data formatting | bytes 1048576 | tf_op jit(solution)/shard_map/reshape | solution.py:186
  211.9 3.1 %fusion.4 = f32[4,64,512]{2,1,0:T(8,128)S(1)} fusion(bf16[4,64,1024]{2,1,0:T(8,128)(2,1)S(1)} %reshape.278, bf16[4,256,512]{2,1,0:T(8,128)(2,1)} %get-tuple-element.20, bf16[4,256,512]{2,1,0:T(8,128)(2,1)} %get-tuple-element.19, bf16[4,256,512]{2,1,0:T(8,128)(2,1)} %fusion.59), kind=kOutput, calls=%fused_computation.11 | convolution fusion | flops 285212672 | bytes 4194304 | tf_op jit(solution)/shard_map/dot_general | solution.py:197
  215.1 0.9 copy.23
  (66 shorter events, 10.8 us)
Async XLA Ops:
  0.0 61.3 %copy-start = (bf16[512,1024]{1,0:T(8,128)(2,1)S(1)}, bf16[512,1024]{1,0:T(8,128)(2,1)}, u32[]{:S(2)}) copy-start(bf16[512,1024]{1,0:T(8,128)(2,1)} %param.5) | copy-start | bytes 3145732
  0.0 12.6 %copy-start.3 = (bf16[64,38912]{1,0:T(8,128)(2,1)S(1)}, bf16[64,38912]{1,0:T(8,128)(2,1)}, u32[]{:S(2)}) copy-start(bf16[64,38912]{1,0:T(8,128)(2,1)} %param.4) | copy-start | bytes 14942212
  14.7 3.5 %copy-start.6 = (bf16[16,64,2048]{2,1,0:T(8,128)(2,1)}, bf16[16,64,2048]{2,1,0:T(8,128)(2,1)S(1)}, u32[]{:S(2)}) copy-start(bf16[16,64,2048]{2,1,0:T(8,128)(2,1)S(1)} %get-tuple-element.5) | copy-start | bytes 12582916
  16.3 11.4 %copy-start.4 = (bf16[16,64,2048]{2,1,0:T(8,128)(2,1)}, bf16[16,64,2048]{2,1,0:T(8,128)(2,1)S(1)}, u32[]{:S(2)}) copy-start(bf16[16,64,2048]{2,1,0:T(8,128)(2,1)S(1)} %get-tuple-element.14) | copy-start | bytes 12582916
  36.5 2.8 %copy-start.5 = (bf16[16,64,2048]{2,1,0:T(8,128)(2,1)S(1)}, bf16[16,64,2048]{2,1,0:T(8,128)(2,1)}, u32[]{:S(2)}) copy-start(bf16[16,64,2048]{2,1,0:T(8,128)(2,1)} %copy-done.4) | copy-start | bytes 12582916
  36.5 4.1 %copy-start.7 = (bf16[16,64,2048]{2,1,0:T(8,128)(2,1)S(1)}, bf16[16,64,2048]{2,1,0:T(8,128)(2,1)}, u32[]{:S(2)}) copy-start(bf16[16,64,2048]{2,1,0:T(8,128)(2,1)} %copy-done.6) | copy-start | bytes 12582916
  51.9 9.3 %copy-start.9 = (s32[512]{0:T(512)S(1)}, s32[512]{0:T(512)}, u32[]{:S(2)}) copy-start(s32[512]{0:T(512)} %param.7) | copy-start | bytes 6148
  53.4 48.5 %all-to-all-start = ((bf16[2,16,32,1024]{3,2,0,1:T(8,128)(2,1)}), bf16[2,16,32,1024]{3,2,0,1:T(8,128)(2,1)}, u32[]{:S(2)}, u32[]{:S(2)}) async-start(bf16[2,16,32,1024]{3,2,0,1:T(8,128)(2,1)} %copy.13), calls=%async_computation | async-start | bytes 4194304 | tf_op jit(solution)/shard_map/all_to_all | solution.py:174
  168.2 0.8 copy-start.2
  171.7 17.7 %copy-start.8 = (s32[256,512]{1,0:T(8,128)S(1)}, s32[256,512]{1,0:T(8,128)}, u32[]{:S(2)}) copy-start(s32[256,512]{1,0:T(8,128)} %param.6) | copy-start | bytes 1572868
  178.1 25.5 %all-to-all-start.1 = ((bf16[16,2,8192]{2,1,0:T(2,128)(2,1)}), bf16[16,2,8192]{2,1,0:T(2,128)(2,1)S(1)}, u32[]{:S(2)}, u32[]{:S(2)}) async-start(bf16[16,2,8192]{2,1,0:T(2,128)(2,1)} %reshape.289), calls=%async_computation.1 | async-start | bytes 1048576 | tf_op jit(solution)/shard_map/all_to_all | solution.py:184
  211.8 4.1 %copy-start.1 = (bf16[512,1024]{1,0:T(8,128)(2,1)S(1)}, bf16[512,1024]{1,0:T(8,128)(2,1)}, u32[]{:S(2)}) copy-start(bf16[512,1024]{1,0:T(8,128)(2,1)} %param.5) | copy-start | bytes 3145732

commit v2 on v1

--- a/solution.py
+++ b/solution.py
@@ -17,6 +17,7 @@
 HALF_ROOT = math.sqrt(0.5)
 ROWS = 16
 COLS = 256
+LANES = 128
 
 
 def prototype():
@@ -72,10 +73,76 @@
     return 1.0 - 2.0 * sine * sine, 2.0 * sine * cosine
 
 
-def beam_kernel(channels, first_ref, steer_ref, x_ref, table_ref, out_ref, weights):
-    group = x_ref.shape[0]
-    frames = x_ref.shape[1] // 2
+def frame_kernel(window_ref, voltages_ref, out_ref):
+    antenna_local, samples = voltages_ref.shape
+    pieces = samples // TRANSFORM_SIZE
+
+    def lane_step(index, carry):
+        start = pl.multiple_of(index * LANES, LANES)
+        window = [window_ref[tap, pl.ds(start, LANES)] for tap in range(POLYPHASE_TAPS)]
+        for row in range(0, antenna_local, ROWS):
+            held = []
+            for piece in range(pieces):
+                lanes = pl.ds(pl.multiple_of(start + piece * TRANSFORM_SIZE, LANES), LANES)
+                held.append(voltages_ref[row : row + ROWS, lanes].astype(jnp.float32))
+                if len(held) == POLYPHASE_TAPS:
+                    total = held[0] * window[0]
+                    for tap in range(1, POLYPHASE_TAPS):
+                        total = total + held[tap] * window[tap]
+                    frame = piece - POLYPHASE_TAPS + 1
+                    first = frame * antenna_local + row
+                    out_ref[first : first + ROWS, pl.ds(start, LANES)] = total.astype(jnp.bfloat16)
+                    held = held[1:]
+        return carry
+
+    lax.fori_loop(0, TRANSFORM_SIZE // LANES, lane_step, 0)
+
+
+def make_frames(window, voltages):
+    antenna_local, samples = voltages.shape
+    frames = samples // TRANSFORM_SIZE - POLYPHASE_TAPS + 1
+    return pl.pallas_call(
+        frame_kernel,
+        out_shape=jax.ShapeDtypeStruct((frames * antenna_local, TRANSFORM_SIZE), jnp.bfloat16),
+        in_specs=[pl.BlockSpec(memory_space=pltpu.VMEM)] * 2,
+        out_specs=pl.BlockSpec(memory_space=pltpu.VMEM),
+        compiler_params=pltpu.CompilerParams(vmem_limit_bytes=40 * 1024 * 1024),
+    )(window, voltages)
+
+
+def beam_kernel(
+    channels, group, frames, first_ref, steer_ref, x_ref, table_ref, out_ref, weights, held
+):
     antennas, beams = steer_ref.shape
+    sources, rows_of_source, _ = x_ref.shape
+    antenna_local = antennas // sources
+
+    @pl.when(pl.program_id(0) == 0)
+    def _():
+        width = min(LANES, antenna_local)
+        per = LANES // width
+        block = lax.broadcasted_iota(jnp.int32, (rows_of_source, LANES), 1) // width
+        for tile in range(antennas // LANES):
+            for lane in range(0, frames * antenna_local, LANES * max(1, antenna_local // LANES)):
+                if per == 1:
+                    source = tile * LANES // antenna_local
+                    offset = lane + tile * LANES % antenna_local
+                    value = x_ref[source, :, offset : offset + LANES].astype(jnp.float32)
+                    held[tile, pl.ds(lane // antenna_local, rows_of_source, stride=frames), :] = value
+                    continue
+                values = [
+                    x_ref[tile * per + i, :, lane : lane + LANES].astype(jnp.float32)
+                    for i in range(per)
+                ]
+                for j in range(per):
+                    total = None
+                    for i in range(per):
+                        shift = (i - j) * width % LANES
+                        value = pltpu.roll(values[i], shift, 1) if shift else values[i]
+                        total = value if total is None else jnp.where(block == i, value, total)
+                    frame = lane // LANES * per + j
+                    held[tile, pl.ds(frame, rows_of_source, stride=frames), :] = total
+
     first = first_ref[0] + pl.program_id(0) * group
     factor = 1.0 + first.astype(jnp.float32) * (1.0 / channels)
 
@@ -103,7 +170,10 @@
     lax.fori_loop(0, antennas // ROWS, rows_step, 0)
 
     def channel_step(slot, carry):
-        x = x_ref[slot]
+        channel = pl.program_id(0) * group + slot
+        spot = pl.ds(pl.multiple_of(channel * 2 * frames, 2 * frames), 2 * frames)
+        x = jnp.concatenate([held[i, spot, :] for i in range(antennas // LANES)], 1)
+        x = x.astype(jnp.bfloat16)
         by_cos = jnp.dot(x, weights[slot, 0], preferred_element_type=jnp.float32)
         by_sin = jnp.dot(x, weights[slot, 1], preferred_element_type=jnp.float32)
         real = by_cos[:frames] + by_sin[frames:]
@@ -117,25 +187,29 @@
     lax.fori_loop(0, group, channel_step, 0)
 
 
-def form_beams(first, steering, spectra, table, channels):
-    chan_local, double_frames, antennas = spectra.shape
-    beams = steering.shape[1]
+def form_beams(first, steering, turned, table, channels, frames):
+    sources, rows_of_source, _ = turned.shape
+    chan_local = rows_of_source // 2
+    antennas, beams = steering.shape
     group = math.gcd(chan_local, 8)
     rows = table.shape[0]
     return pl.pallas_call(
-        functools.partial(beam_kernel, channels),
+        functools.partial(beam_kernel, channels, group, frames),
         grid=(chan_local // group,),
         out_shape=jax.ShapeDtypeStruct((chan_local, rows, beams), jnp.bfloat16),
         in_specs=[
             pl.BlockSpec(memory_space=pltpu.SMEM),
             pl.BlockSpec((antennas, beams), lambda i: (0, 0)),
-            pl.BlockSpec((group, double_frames, antennas), lambda i: (i, 0, 0)),
+            pl.BlockSpec(turned.shape, lambda i: (0, 0, 0)),
             pl.BlockSpec(table.shape, lambda i: (0, 0)),
         ],
         out_specs=pl.BlockSpec((group, rows, beams), lambda i: (i, 0, 0)),
-        scratch_shapes=[pltpu.VMEM((group, 2, antennas, beams), jnp.bfloat16)],
+        scratch_shapes=[
+            pltpu.VMEM((group, 2, antennas, beams), jnp.bfloat16),
+            pltpu.VMEM((antennas // LANES, rows_of_source * frames, LANES), jnp.float32),
+        ],
         compiler_params=pltpu.CompilerParams(vmem_limit_bytes=40 * 1024 * 1024),
-    )(first, steering, spectra, table)
+    )(first, steering, turned, table)
 
 
 def shards(voltages, steering_delays, trial_delays, beam_order):
@@ -149,35 +223,23 @@
     chan_local = channels // devices
     beam_local = beams // devices
 
-    window = prototype()
-    pieces = [
-        voltages[:, i * TRANSFORM_SIZE : (i + 1) * TRANSFORM_SIZE]
-        for i in range(all_frames + POLYPHASE_TAPS - 1)
-    ]
-    stacked = jnp.stack(pieces, 0)
-    frames = stacked[:all_frames] * window[0]
-    for tap in range(1, POLYPHASE_TAPS):
-        frames = frames + stacked[tap : tap + all_frames] * window[tap]
-    frame_rows = frames.astype(jnp.bfloat16).reshape(all_frames * antenna_local, TRANSFORM_SIZE)
-
-    channel_ids = jnp.arange(channels, dtype=jnp.int32)
+    frame_rows = make_frames(prototype(), voltages)
+    row_ids = jnp.arange(2 * channels, dtype=jnp.int32)
     sample = jnp.arange(TRANSFORM_SIZE, dtype=jnp.int32)
-    turns = channel_ids[:, None] * sample[None, :] & (TRANSFORM_SIZE - 1)
-    phase_turns = turns.astype(jnp.float32) * (1.0 / TRANSFORM_SIZE)
-    cosine, sine = cos_sin_turns(phase_turns)
-    filter_rows = jnp.stack([cosine.astype(jnp.bfloat16), (-sine).astype(jnp.bfloat16)], 0)
-    filter_rows = filter_rows.reshape(2 * channels, TRANSFORM_SIZE)
+    turns = (row_ids >> 1)[:, None] * sample[None, :] + ((row_ids & 1) * (TRANSFORM_SIZE // 4))[:, None]
+    turns = ((turns + TRANSFORM_SIZE // 2) & (TRANSFORM_SIZE - 1)) - TRANSFORM_SIZE // 2
+    half = turns.astype(jnp.float32) * (math.pi / TRANSFORM_SIZE)
+    half_sine = half * polynomial(half * half, SIN_TERMS)
+    filter_rows = (1.0 - 2.0 * half_sine * half_sine).astype(jnp.bfloat16)
     spectra = lax.dot_general(
         filter_rows, frame_rows, (((1,), (1,)), ((), ())), preferred_element_type=jnp.float32
     ).astype(jnp.bfloat16)
-    spectra = spectra.reshape(2, devices, chan_local, all_frames * antenna_local)
-    turned = lax.all_to_all(spectra, "chan", split_axis=1, concat_axis=1, tiled=True)
-    turned = turned.reshape(2, devices, chan_local, all_frames, antenna_local)
-    turned = turned.transpose(2, 0, 3, 1, 4).reshape(chan_local, 2 * all_frames, antennas)
+    spectra = spectra.reshape(devices, 2 * chan_local, all_frames * antenna_local)
+    turned = lax.all_to_all(spectra, "chan", split_axis=0, concat_axis=0, tiled=True)
 
     steering = steering_delays[beam_order].T
     first = (device * chan_local).astype(jnp.int32).reshape(1)
-    fluctuation = form_beams(first, steering, turned, time_table(blocks), channels)
+    fluctuation = form_beams(first, steering, turned, time_table(blocks), channels, all_frames)
 
     outgoing = fluctuation.reshape(chan_local, 2 * FLUCT_BINS * blocks, devices, beam_local)
     outgoing = outgoing.transpose(2, 1, 3, 0)

time: 217 us -> 171 us (0.79)
  local copies, waits for them, and re-layouts: 70.1 us -> 30.9 us
  other arithmetic: 25.4 us -> 6.93 us
  matrix products: 7.91 us -> 17.6 us
  Pallas kernels: 46 us -> 50.7 us
  waiting for transfers between devices: 46.7 us -> 44.3 us
    unnamed x73 -> x18, local copies, waits for them, and re-layouts: 29.3 us -> 12.1 us
    convert_element_type x3 -> x0, other arithmetic: 16.5 us -> none  [the longest x1 6.57 us: shards(): frames.astype(jnp.bfloat16)]
    reshape x3 -> x0, local copies, waits for them, and re-layouts: 10.9 us -> none  [the longest x1 5.47 us: shards(): turned.transpose(2, 0, 3, 1, 4)]
    transpose x1 -> x0, local copies, waits for them, and re-layouts: 9.03 us -> none  [shards(): turned.transpose(2, 0, 3, 1, 4)]
    dot_general x1, matrix products: 4.77 us -> 11.9 us  [shards(): lax.dot_general(filter_rows, frame_rows, (((1,), (1,)), ((), ())), prefer...]
    pallas_call x1 -> x2, Pallas kernels: 46 us -> 50.7 us  [the longest x1 48.1 us: form_beams(): pl.pallas_call(functools.partial(beam_kernel, channels, group, frames), g...]
    another operation x4 -> x0, local copies, waits for them, and re-layouts: 3.71 us -> none  [shards(): stacked = jnp.stack(pieces, 0)]
    dot_general x1, matrix products: 3.14 us -> 5.63 us  [shards(): lax.dot_general(parts, both, (((2,), (2,)), ((0,), (0,))), preferred_elem...]
  transfers between devices with their start and end apart: 2 -> 2, of which waited for: 2 -> 2; matrix products, arithmetic and copies ran while one was open for 4% -> 6% of each run, Pallas kernels for 0% -> 0%
where the time goes in v2:
time: 171 us; the launch traced here: 170 us
  Pallas kernels  50.7 us (30%)
  waiting for transfers between devices  44.3 us (26%)
  local copies, waits for them, and re-layouts  30.9 us (18%)
  starting transfers between devices  18.8 us (11%)
  matrix products  17.6 us (10%)
  other arithmetic  6.93 us (4%)
    pallas_call x1, Pallas kernels, form_beams(): pl.pallas_call(functools.partial(beam_kernel, channels, group, frames), g...  48.1 us
    all_to_all x1, waiting for transfers between devices, shards(): lax.all_to_all(spectra, 'chan', split_axis=0, concat_axis=0, tiled=True)  35.6 us
    unnamed x18, local copies, waits for them, and re-layouts  12.1 us
    dot_general x1, matrix products, shards(): lax.dot_general(filter_rows, frame_rows, (((1,), (1,)), ((), ())), prefer...  11.9 us
    all_to_all x1, starting transfers between devices, shards(): lax.all_to_all(outgoing, 'chan', split_axis=0, concat_axis=0, tiled=True)  11.3 us
    all_to_all x1, waiting for transfers between devices, shards(): lax.all_to_all(outgoing, 'chan', split_axis=0, concat_axis=0, tiled=True)  8.75 us
    all_to_all x1, starting transfers between devices, shards(): lax.all_to_all(spectra, 'chan', split_axis=0, concat_axis=0, tiled=True)  7.55 us
    dot_general x1, matrix products, shards(): lax.dot_general(parts, both, (((2,), (2,)), ((0,), (0,))), preferred_elem...  5.63 us
  transfers between devices with their start and end apart: 2, of which 2 were waited for; matrix products, arithmetic and copies ran while one was open for 6% of the time, Pallas kernels for 0%

profile of v2, /device:TPU:0, one launch (start us, length us, event | category | flops | bytes accessed | tf_op | source)
XLA Modules:
  0.0 170.0 jit_solution(1783760926124435108)
XLA Ops:
  0.0 0.0 copy-start
  0.0 0.8 fusion.84
  1.5 0.3 fusion.58.window_ref
  1.8 0.0 copy-start.1
  1.8 2.4 %copy-done.1 = bf16[64,38912]{1,0:T(8,128)(2,1)S(1)} copy-done((bf16[64,38912]{1,0:T(8,128)(2,1)S(1)}, bf16[64,38912]{1,0:T(8,128)(2,1)}, u32[]{:S(2)}) %copy-start.1) | copy-done | bytes 4980760
  4.2 2.6 %shard_map.46 = bf16[1024,2048]{1,0:T(8,128)(2,1)S(1)} custom-call(f32[4,2048]{1,0:T(4,128)S(1)} %fusion.58.window_ref, bf16[64,38912]{1,0:T(8,128)(2,1)S(1)} %copy-done.1), custom_call_target="tpu_custom_call" | custom-call | tf_op jit(solution)/shard_map/pallas_call | solution.py:104
  6.8 11.9 %fusion.38 = bf16[1024,1024]{1,0:T(8,128)(2,1)} fusion(bf16[1024,2048]{1,0:T(8,128)(2,1)S(1)} %shard_map.46, s32[1024]{0:T(1024)S(1)} %get-tuple-element.9, s32[1024]{0:T(1024)S(1)} %get-tuple-element.10), kind=kOutput, calls=%fused_computation.49 | convolution fusion | flops 4348444672 | bytes 6299648 | tf_op jit(solution)/shard_map/dot_general | solution.py:234
  18.8 0.0 copy-start.7
  18.8 7.6 %all-to-all-start = ((bf16[16,64,1024]{2,1,0:T(8,128)(2,1)}), bf16[16,64,1024]{2,1,0:T(8,128)(2,1)S(1)}, u32[]{:S(2)}, u32[]{:S(2)}) async-start(bf16[16,64,1024]{2,1,0:T(8,128)(2,1)} %bitcast.26), calls=%async_computation | async-start | bytes 4194304 | tf_op jit(solution)/shard_map/all_to_all | solution.py:238
  26.4 0.1 fusion.88
  26.5 0.1 multiply_convert_fusion
  26.6 0.1 convert_element_type.43.table_ref
  26.7 0.0 copy-done.7
  26.7 0.0 copy-done
  26.7 2.8 %gather_fusion = bf16[512,1024]{1,0:T(8,128)(2,1)} fusion(bf16[512,1024]{1,0:T(8,128)(2,1)S(1)} %copy-done, s32[1024]{0:T(1024)S(1)} %pad_clamp_fusion), kind=kCustom, calls=%fused_computation | custom fusion | bytes 2099200 | tf_op jit(solution)/shard_map/gather | solution.py:240
  29.5 2.3 %copy.8 = bf16[512,1024]{0,1:T(8,128)(2,1)} copy(bf16[512,1024]{1,0:T(8,128)(2,1)} %gather_fusion) | data formatting | bytes 2097152 | tf_op jit(solution)/shard_map/gather | solution.py:240
  31.8 35.6 %all-to-all-done.x_ref = bf16[16,64,1024]{2,1,0:T(8,128)(2,1)S(1)} async-done(((bf16[16,64,1024]{2,1,0:T(8,128)(2,1)}), bf16[16,64,1024]{2,1,0:T(8,128)(2,1)S(1)}, u32[]{:S(2)}, u32[]{:S(2)}) %all-to-all-start) | async-done | bytes 2097184 | tf_op jit(solution)/shard_map/all_to_all | solution.py:238
  67.3 0.0 copy-start.2
  67.3 1.2 copy-done.2
  68.6 48.1 %shard_map.47 = bf16[32,16,512]{2,1,0:T(8,128)(2,1)S(1)} custom-call(s32[1]{0:T(128)} %bitcast.first_ref, bf16[1024,512]{1,0:T(8,128)(2,1)S(1)} %bitcast.22, bf16[16,64,1024]{2,1,0:T(8,128)(2,1)S(1)} %all-to-all-done.x_ref, bf16[16,16]{1,0:T(8,128)(2,1)S(1)} %convert_element_type.43.table_ref), custom_call_target="tpu_custom_call" | custom-call | tf_op jit(solution)/shard_map/pallas_call | solution.py:196
  116.7 0.0 copy-start.3
  116.7 0.8 copy-done.3
  117.5 2.7 %reshape.56 = bf16[32,16,16,32]{3,2,1,0:T(8,128)(2,1)S(1)} reshape(bf16[32,16,512]{2,1,0:T(8,128)(2,1)} %copy-done.3) | data formatting | bytes 1048576 | tf_op jit(solution)/shard_map/reshape | solution.py:244
  120.2 1.9 %copy.17 = bf16[32,16,16,32]{3,1,0,2:T(8,128)(2,1)} copy(bf16[32,16,16,32]{3,2,1,0:T(8,128)(2,1)S(1)} %reshape.56) | data formatting | bytes 1048576 | tf_op jit(solution)/shard_map/reshape | solution.py:244
  122.1 0.0 copy-start.4
  122.1 4.6 %reshape.69 = bf16[16,2,8192]{2,1,0:T(2,128)(2,1)} reshape(bf16[16,32,16,32]{3,2,1,0:T(8,128)(2,1)} %bitcast.23) | data formatting | bytes 1048576
  126.7 11.3 %all-to-all-start.1 = ((bf16[16,2,8192]{2,1,0:T(2,128)(2,1)}), bf16[16,2,8192]{2,1,0:T(2,128)(2,1)}, u32[]{:S(2)}, u32[]{:S(2)}) async-start(bf16[16,2,8192]{2,1,0:T(2,128)(2,1)} %reshape.69), calls=%async_computation.1 | async-start | bytes 1048576 | tf_op jit(solution)/shard_map/all_to_all | solution.py:246
  138.0 0.0 copy-done.4
  138.0 2.2 %fusion.102 = bf16[4,256,512]{2,1,0:T(8,128)(2,1)} fusion(s32[256,512]{1,0:T(8,128)S(1)} %copy-done.4, s32[4]{0:T(128)S(1)} %iota_add_fusion.1), kind=kLoop, calls=%fused_computation.146 | loop fusion | flops 10485760 | bytes 1572880 | tf_op jit(solution)/shard_map/neg | solution.py:254
  140.2 3.3 %add_convert_fusion = (bf16[4,256,512]{2,1,0:T(8,128)(2,1)}, bf16[4,256,512]{2,1,0:T(8,128)(2,1)}) fusion(s32[256,512]{1,0:T(8,128)S(1)} %copy-done.4, s32[4]{0:T(128)S(1)} %iota_add_fusion.1), kind=kLoop, calls=%fused_computation.38 | loop fusion | flops 15728640 | bytes 2621456 | tf_op jit(solution)/shard_map/convert_element_type | solution.py:52
  143.5 8.7 %all-to-all-done.1 = bf16[16,2,8192]{2,1,0:T(2,128)(2,1)} async-done(((bf16[16,2,8192]{2,1,0:T(2,128)(2,1)}), bf16[16,2,8192]{2,1,0:T(2,128)(2,1)}, u32[]{:S(2)}, u32[]{:S(2)}) %all-to-all-start.1) | async-done | bytes 524320 | tf_op jit(solution)/shard_map/all_to_all | solution.py:246
  152.3 3.1 %reshape.70 = bf16[16,32,16,32]{3,2,1,0:T(8,128)(2,1)S(1)} reshape(bf16[16,2,8192]{2,1,0:T(2,128)(2,1)} %all-to-all-done.1) | data formatting | bytes 1048576
  155.3 3.7 %copy.10 = bf16[16,2,2,4,32,32]{5,0,2,4,1,3:T(8,128)(2,1)} copy(bf16[16,2,2,4,32,32]{4,3,2,1,5,0:T(4,128)(2,1)S(1)} %bitcast.24) | data formatting | bytes 1048576 | tf_op jit(solution)/shard_map/reshape | solution.py:247
  159.1 0.0 copy-start.5
  159.1 0.0 copy-start.6
  159.1 4.4 %reshape.58 = bf16[4,64,1024]{2,1,0:T(8,128)(2,1)} reshape(bf16[4,2,32,2,16,32]{5,4,3,2,1,0:T(8,128)(2,1)} %bitcast.25) | data formatting | bytes 1048576 | tf_op jit(solution)/shard_map/reshape | solution.py:248
  163.5 0.0 copy-done.5
  163.5 0.0 copy-done.6
  163.5 5.6 %fusion.8 = f32[4,64,512]{2,1,0:T(8,128)S(1)} fusion(bf16[4,64,1024]{2,1,0:T(8,128)(2,1)} %reshape.58, bf16[4,256,512]{2,1,0:T(8,128)(2,1)} %get-tuple-element.6, bf16[4,256,512]{2,1,0:T(8,128)(2,1)S(1)} %copy-done.6, bf16[4,256,512]{2,1,0:T(8,128)(2,1)S(1)} %copy-done.5), kind=kOutput, calls=%fused_computation.15 | convolution fusion | flops 285212672 | bytes 4194304 | tf_op jit(solution)/shard_map/dot_general | solution.py:259
  169.2 0.9 copy.16
  (7 shorter events, 0.1 us)
Async XLA Ops:
  0.0 26.7 %copy-start = (bf16[512,1024]{1,0:T(8,128)(2,1)S(1)}, bf16[512,1024]{1,0:T(8,128)(2,1)}, u32[]{:S(2)}) copy-start(bf16[512,1024]{1,0:T(8,128)(2,1)} %param.5) | copy-start | bytes 3145732
  1.8 2.4 %copy-start.1 = (bf16[64,38912]{1,0:T(8,128)(2,1)S(1)}, bf16[64,38912]{1,0:T(8,128)(2,1)}, u32[]{:S(2)}) copy-start(bf16[64,38912]{1,0:T(8,128)(2,1)} %voltages_ref.1) | copy-start | bytes 14942212
  18.8 7.9 %copy-start.7 = (s32[512]{0:T(512)S(1)}, s32[512]{0:T(512)}, u32[]{:S(2)}) copy-start(s32[512]{0:T(512)} %param.7) | copy-start | bytes 6148
  18.8 48.5 %all-to-all-start = ((bf16[16,64,1024]{2,1,0:T(8,128)(2,1)}), bf16[16,64,1024]{2,1,0:T(8,128)(2,1)S(1)}, u32[]{:S(2)}, u32[]{:S(2)}) async-start(bf16[16,64,1024]{2,1,0:T(8,128)(2,1)} %bitcast.26), calls=%async_computation | async-start | bytes 4194304 | tf_op jit(solution)/shard_map/all_to_all | solution.py:238
  67.3 1.2 copy-start.2
  116.7 0.8 copy-start.3
  122.1 15.9 %copy-start.4 = (s32[256,512]{1,0:T(8,128)S(1)}, s32[256,512]{1,0:T(8,128)}, u32[]{:S(2)}) copy-start(s32[256,512]{1,0:T(8,128)} %param.6) | copy-start | bytes 1572868
  126.7 25.6 %all-to-all-start.1 = ((bf16[16,2,8192]{2,1,0:T(2,128)(2,1)}), bf16[16,2,8192]{2,1,0:T(2,128)(2,1)}, u32[]{:S(2)}, u32[]{:S(2)}) async-start(bf16[16,2,8192]{2,1,0:T(2,128)(2,1)} %reshape.69), calls=%async_computation.1 | async-start | bytes 1048576 | tf_op jit(solution)/shard_map/all_to_all | solution.py:246
  159.1 4.4 %copy-start.5 = (bf16[4,256,512]{2,1,0:T(8,128)(2,1)S(1)}, bf16[4,256,512]{2,1,0:T(8,128)(2,1)}, u32[]{:S(2)}) copy-start(bf16[4,256,512]{2,1,0:T(8,128)(2,1)} %fusion.102) | copy-start | bytes 3145732
  159.1 4.4 %copy-start.6 = (bf16[4,256,512]{2,1,0:T(8,128)(2,1)S(1)}, bf16[4,256,512]{2,1,0:T(8,128)(2,1)}, u32[]{:S(2)}) copy-start(bf16[4,256,512]{2,1,0:T(8,128)(2,1)} %get-tuple-element.5) | copy-start | bytes 3145732

commit v3 on v2

--- a/solution.py
+++ b/solution.py
@@ -111,27 +111,66 @@
 
 
 def beam_kernel(
-    channels, group, frames, first_ref, steer_ref, x_ref, table_ref, out_ref, weights, held
+    channels, steer_ref, x_ref, table_ref, out_ref,
+    weights, held, arrived, send_sem, recv_sem, own_sem,
 ):
     antennas, beams = steer_ref.shape
-    sources, rows_of_source, _ = x_ref.shape
+    sources, chunks, rows_of_chunk, width_of_source = x_ref.shape
+    group = rows_of_chunk // 2
     antenna_local = antennas // sources
-
-    @pl.when(pl.program_id(0) == 0)
-    def _():
+    frames = width_of_source // antenna_local
+    me = lax.axis_index("chan")
+
+    def greet(distance, carry):
+        peer = lax.rem(me + distance, sources)
+        pl.semaphore_signal(
+            barrier, inc=1, device_id={"chan": peer}, device_id_type=pl.DeviceIdType.MESH
+        )
+        return carry
+
+    barrier = pltpu.get_barrier_semaphore()
+    lax.fori_loop(1, sources, greet, 0)
+    pl.semaphore_wait(barrier, sources - 1)
+
+    def to_peer(chunk, distance):
+        peer = lax.rem(me + distance, sources)
+        return pltpu.make_async_remote_copy(
+            src_ref=x_ref.at[peer, chunk],
+            dst_ref=arrived.at[chunk, me],
+            send_sem=send_sem.at[chunk, distance - 1],
+            recv_sem=recv_sem.at[chunk, distance - 1],
+            device_id={"chan": peer},
+            device_id_type=pl.DeviceIdType.MESH,
+        )
+
+    def own(chunk):
+        return pltpu.make_async_copy(x_ref.at[me, chunk], arrived.at[chunk, me], own_sem.at[chunk])
+
+    def send_chunk(chunk, carry):
+        def send(distance, inner):
+            to_peer(chunk, distance).start()
+            return inner
+
+        lax.fori_loop(1, sources, send, 0)
+        own(chunk).start()
+        return carry
+
+    lax.fori_loop(0, chunks, send_chunk, 0)
+
+    def arrange(chunk):
         width = min(LANES, antenna_local)
         per = LANES // width
-        block = lax.broadcasted_iota(jnp.int32, (rows_of_source, LANES), 1) // width
+        block = lax.broadcasted_iota(jnp.int32, (rows_of_chunk, LANES), 1) // width
         for tile in range(antennas // LANES):
             for lane in range(0, frames * antenna_local, LANES * max(1, antenna_local // LANES)):
                 if per == 1:
                     source = tile * LANES // antenna_local
                     offset = lane + tile * LANES % antenna_local
-                    value = x_ref[source, :, offset : offset + LANES].astype(jnp.float32)
-                    held[tile, pl.ds(lane // antenna_local, rows_of_source, stride=frames), :] = value
+                    value = arrived[chunk, source, :, offset : offset + LANES].astype(jnp.float32)
+                    held[tile, pl.ds(lane // antenna_local, rows_of_chunk, stride=frames), :] = value
                     continue
                 values = [
-                    x_ref[tile * per + i, :, lane : lane + LANES].astype(jnp.float32)
+                    arrived[chunk, tile * per + i, :, lane : lane + LANES].astype(jnp.float32)
                     for i in range(per)
                 ]
                 for j in range(per):
@@ -141,12 +180,9 @@
                         value = pltpu.roll(values[i], shift, 1) if shift else values[i]
                         total = value if total is None else jnp.where(block == i, value, total)
                     frame = lane // LANES * per + j
-                    held[tile, pl.ds(frame, rows_of_source, stride=frames), :] = total
-
-    first = first_ref[0] + pl.program_id(0) * group
-    factor = 1.0 + first.astype(jnp.float32) * (1.0 / channels)
-
-    def rows_step(index, carry):
+                    held[tile, pl.ds(frame, rows_of_chunk, stride=frames), :] = total
+
+    def rows_step(factor, index):
         rows = pl.ds(pl.multiple_of(index * ROWS, ROWS), ROWS)
         for start in range(0, beams, COLS):
             cols = pl.ds(start, COLS)
@@ -165,13 +201,9 @@
                 if slot + 1 < group:
                     cosine, cos_before = double * cosine - cos_before, cosine
                     sine, sin_before = double * sine - sin_before, sine
-        return carry
-
-    lax.fori_loop(0, antennas // ROWS, rows_step, 0)
-
-    def channel_step(slot, carry):
-        channel = pl.program_id(0) * group + slot
-        spot = pl.ds(pl.multiple_of(channel * 2 * frames, 2 * frames), 2 * frames)
+
+    def channel_step(chunk, slot):
+        spot = pl.ds(pl.multiple_of(slot * 2 * frames, 2 * frames), 2 * frames)
         x = jnp.concatenate([held[i, spot, :] for i in range(antennas // LANES)], 1)
         x = x.astype(jnp.bfloat16)
         by_cos = jnp.dot(x, weights[slot, 0], preferred_element_type=jnp.float32)
@@ -179,42 +211,74 @@
         real = by_cos[:frames] + by_sin[frames:]
         imag = by_cos[frames:] - by_sin[:frames]
         intensity = (real * real + imag * imag).astype(jnp.bfloat16)
-        out_ref[slot] = jnp.dot(
+        out_ref[chunk * group + slot] = jnp.dot(
             table_ref[...], intensity, preferred_element_type=jnp.float32
         ).astype(jnp.bfloat16)
+
+    def chunk_step(chunk, carry):
+        first = (me * chunks + chunk) * group
+        factor = 1.0 + first.astype(jnp.float32) * (1.0 / channels)
+
+        def rows_loop(index, inner):
+            rows_step(factor, index)
+            return inner
+
+        def wait(distance, inner):
+            to_peer(chunk, distance).wait_recv()
+            return inner
+
+        def channel_loop(slot, inner):
+            channel_step(chunk, slot)
+            return inner
+
+        lax.fori_loop(0, antennas // ROWS, rows_loop, 0)
+        lax.fori_loop(1, sources, wait, 0)
+        own(chunk).wait()
+        arrange(chunk)
+        lax.fori_loop(0, group, channel_loop, 0)
         return carry
 
-    lax.fori_loop(0, group, channel_step, 0)
-
-
-def form_beams(first, steering, turned, table, channels, frames):
-    sources, rows_of_source, _ = turned.shape
+    lax.fori_loop(0, chunks, chunk_step, 0)
+
+    def sent_chunk(chunk, carry):
+        def sent(distance, inner):
+            to_peer(chunk, distance).wait_send()
+            return inner
+
+        return lax.fori_loop(1, sources, sent, carry)
+
+    lax.fori_loop(0, chunks, sent_chunk, 0)
+
+
+def form_beams(steering, spectra, table, channels):
+    sources, rows_of_source, width = spectra.shape
     chan_local = rows_of_source // 2
     antennas, beams = steering.shape
+    frames = width * sources // antennas
     group = math.gcd(chan_local, 8)
+    chunks = chan_local // group
     rows = table.shape[0]
     return pl.pallas_call(
-        functools.partial(beam_kernel, channels, group, frames),
-        grid=(chan_local // group,),
+        functools.partial(beam_kernel, channels),
         out_shape=jax.ShapeDtypeStruct((chan_local, rows, beams), jnp.bfloat16),
-        in_specs=[
-            pl.BlockSpec(memory_space=pltpu.SMEM),
-            pl.BlockSpec((antennas, beams), lambda i: (0, 0)),
-            pl.BlockSpec(turned.shape, lambda i: (0, 0, 0)),
-            pl.BlockSpec(table.shape, lambda i: (0, 0)),
-        ],
-        out_specs=pl.BlockSpec((group, rows, beams), lambda i: (i, 0, 0)),
+        in_specs=[pl.BlockSpec(memory_space=pltpu.VMEM)] * 3,
+        out_specs=pl.BlockSpec(memory_space=pltpu.VMEM),
         scratch_shapes=[
             pltpu.VMEM((group, 2, antennas, beams), jnp.bfloat16),
-            pltpu.VMEM((antennas // LANES, rows_of_source * frames, LANES), jnp.float32),
+            pltpu.VMEM((antennas // LANES, 2 * group * frames, LANES), jnp.float32),
+            pltpu.VMEM((chunks, sources, 2 * group, width), jnp.bfloat16),
+            pltpu.SemaphoreType.DMA((chunks, sources - 1)),
+            pltpu.SemaphoreType.DMA((chunks, sources - 1)),
+            pltpu.SemaphoreType.DMA((chunks,)),
         ],
-        compiler_params=pltpu.CompilerParams(vmem_limit_bytes=40 * 1024 * 1024),
-    )(first, steering, turned, table)
+        compiler_params=pltpu.CompilerParams(
+            vmem_limit_bytes=40 * 1024 * 1024, collective_id=0, has_side_effects=True
+        ),
+    )(steering, spectra.reshape(sources, chunks, 2 * group, width), table)
 
 
 def shards(voltages, steering_delays, trial_delays, beam_order):
     devices = lax.axis_size("chan")
-    device = lax.axis_index("chan")
     antenna_local, samples = voltages.shape
     beams, antennas = steering_delays.shape
     trials, channels = trial_delays.shape
@@ -235,11 +299,8 @@
         filter_rows, frame_rows, (((1,), (1,)), ((), ())), preferred_element_type=jnp.float32
     ).astype(jnp.bfloat16)
     spectra = spectra.reshape(devices, 2 * chan_local, all_frames * antenna_local)
-    turned = lax.all_to_all(spectra, "chan", split_axis=0, concat_axis=0, tiled=True)
-
     steering = steering_delays[beam_order].T
-    first = (device * chan_local).astype(jnp.int32).reshape(1)
-    fluctuation = form_beams(first, steering, turned, time_table(blocks), channels, all_frames)
+    fluctuation = form_beams(steering, spectra, time_table(blocks), channels)
 
     outgoing = fluctuation.reshape(chan_local, 2 * FLUCT_BINS * blocks, devices, beam_local)
     outgoing = outgoing.transpose(2, 1, 3, 0)

time: 171 us -> 137 us (0.80)
  waiting for transfers between devices: 44.3 us -> 7.71 us
  Pallas kernels: 50.7 us -> 64.5 us
  local copies, waits for them, and re-layouts: 30.9 us -> 24.1 us
  starting transfers between devices: 18.8 us -> 13 us
  other arithmetic: 6.93 us -> 8.65 us
    all_to_all x1 -> x0, waiting for transfers between devices: 35.6 us -> none  [shards(): lax.all_to_all(spectra, 'chan', split_axis=0, concat_axis=0, tiled=True)]
    pallas_call x1, Pallas kernels: 48.1 us -> 61.9 us  [form_beams(): pl.pallas_call(functools.partial(beam_kernel, channels), out_shape=jax.Sh...]
    all_to_all x1 -> x0, starting transfers between devices: 7.55 us -> none  [shards(): lax.all_to_all(spectra, 'chan', split_axis=0, concat_axis=0, tiled=True)]
    unnamed x18 -> x12, local copies, waits for them, and re-layouts: 12.1 us -> 8.13 us
    gather x2, local copies, waits for them, and re-layouts: 5.06 us -> 2.6 us  [shards(): steering = steering_delays[beam_order].T]
  transfers between devices with their start and end apart: 2 -> 1, of which waited for: 2 -> 1; matrix products, arithmetic and copies ran while one was open for 6% -> 5% of each run, Pallas kernels for 0% -> 0%
where the time goes in v3:
time: 137 us
  Pallas kernels  64.5 us (47%)
  local copies, waits for them, and re-layouts  24.1 us (18%)
  matrix products  18.3 us (13%)
  starting transfers between devices  13 us (9%)
  other arithmetic  8.65 us (6%)
  waiting for transfers between devices  7.71 us (6%)
    pallas_call x1, Pallas kernels, form_beams(): pl.pallas_call(functools.partial(beam_kernel, channels), out_shape=jax.Sh...  61.9 us
    all_to_all x1, starting transfers between devices, shards(): lax.all_to_all(outgoing, 'chan', split_axis=0, concat_axis=0, tiled=True)  13 us
    dot_general x1, matrix products, shards(): lax.dot_general(filter_rows, frame_rows, (((1,), (1,)), ((), ())), prefer...  12.6 us
    unnamed x12, local copies, waits for them, and re-layouts  8.13 us
    all_to_all x1, waiting for transfers between devices, shards(): lax.all_to_all(outgoing, 'chan', split_axis=0, concat_axis=0, tiled=True)  7.71 us
    dot_general x1, matrix products, shards(): lax.dot_general(parts, both, (((2,), (2,)), ((0,), (0,))), preferred_elem...  5.63 us
    reshape x1, local copies, waits for them, and re-layouts, shards(): exchanged.transpose(3, 1, 4, 2, 0, 5)  4.38 us
    reshape x2, local copies, waits for them, and re-layouts, shards(): fluctuation.reshape(chan_local, 2 * FLUCT_BINS * blocks, devices, beam_lo...  4.37 us
  transfers between devices with their start and end apart: 1, of which 1 were waited for; matrix products, arithmetic and copies ran while one was open for 5% of the time, Pallas kernels for 0%

profile of v3, /device:TPU:0, one launch (start us, length us, event | category | flops | bytes accessed | tf_op | source)
XLA Modules:
  0.0 137.0 jit_solution(8018233136934426229)
XLA Ops:
  0.0 0.0 copy-start
  0.0 0.8 fusion.84
  0.8 0.1 fusion.88
  0.9 0.1 multiply_convert_fusion
  1.0 0.1 convert_element_type.43.table_ref
  1.8 0.3 fusion.58.window_ref
  2.1 0.7 compare_select_fusion.2
  2.8 0.0 copy-done
  2.8 2.1 %gather_fusion = bf16[512,1024]{1,0:T(8,128)(2,1)S(1)} fusion(bf16[512,1024]{1,0:T(8,128)(2,1)S(1)} %copy-done, s32[1024]{0:T(1024)S(1)} %pad_clamp_fusion), kind=kCustom, calls=%fused_computation | custom fusion | bytes 2099200 | tf_op jit(solution)/shard_map/gather | solution.py:302
  4.9 0.5 copy.8
  5.4 0.0 copy-start.1
  5.5 2.4 %copy-done.1 = bf16[64,38912]{1,0:T(8,128)(2,1)S(1)} copy-done((bf16[64,38912]{1,0:T(8,128)(2,1)S(1)}, bf16[64,38912]{1,0:T(8,128)(2,1)}, u32[]{:S(2)}) %copy-start.1) | copy-done | bytes 4980760
  7.9 2.6 %shard_map.46 = bf16[1024,2048]{1,0:T(8,128)(2,1)S(1)} custom-call(f32[4,2048]{1,0:T(4,128)S(1)} %fusion.58.window_ref, bf16[64,38912]{1,0:T(8,128)(2,1)S(1)} %copy-done.1), custom_call_target="tpu_custom_call" | custom-call | tf_op jit(solution)/shard_map/pallas_call | solution.py:104
  10.5 12.6 %fusion.38 = bf16[1024,1024]{1,0:T(8,128)(2,1)S(1)} fusion(bf16[1024,2048]{1,0:T(8,128)(2,1)S(1)} %shard_map.46, s32[1024]{0:T(1024)S(1)} %get-tuple-element.9, s32[1024]{0:T(1024)S(1)} %get-tuple-element.10), kind=kOutput, calls=%fused_computation.49 | convolution fusion | flops 4348444672 | bytes 6299648 | tf_op jit(solution)/shard_map/dot_general | solution.py:298
  23.1 61.9 %shard_map.47 = bf16[32,16,512]{2,1,0:T(8,128)(2,1)S(1)} custom-call(bf16[1024,512]{1,0:T(8,128)(2,1)S(1)} %bitcast.21, bf16[16,4,16,1024]{3,2,1,0:T(8,128)(2,1)S(1)} %bitcast.22, bf16[16,16]{1,0:T(8,128)(2,1)S(1)} %convert_element_type.43.table_ref), custom_call_target="tpu_custom_call" | custom-call | tf_op jit(solution)/shard_map/pallas_call | solution.py:261
  85.0 2.2 %reshape.48 = bf16[32,16,16,32]{3,2,1,0:T(8,128)(2,1)} reshape(bf16[32,16,512]{2,1,0:T(8,128)(2,1)S(1)} %shard_map.47) | data formatting | bytes 1048576 | tf_op jit(solution)/shard_map/reshape | solution.py:305
  87.3 2.1 %copy.17 = bf16[32,16,16,32]{3,1,0,2:T(8,128)(2,1)S(1)} copy(bf16[32,16,16,32]{3,2,1,0:T(8,128)(2,1)} %reshape.48) | data formatting | bytes 1048576 | tf_op jit(solution)/shard_map/reshape | solution.py:305
  89.4 2.6 %reshape.61 = bf16[16,2,8192]{2,1,0:T(2,128)(2,1)} reshape(bf16[16,32,16,32]{3,2,1,0:T(8,128)(2,1)S(1)} %bitcast.23) | data formatting | bytes 1048576
  92.1 0.0 copy-start.2
  92.1 13.0 %all-to-all-start = ((bf16[16,2,8192]{2,1,0:T(2,128)(2,1)}), bf16[16,2,8192]{2,1,0:T(2,128)(2,1)}, u32[]{:S(2)}, u32[]{:S(2)}) async-start(bf16[16,2,8192]{2,1,0:T(2,128)(2,1)} %reshape.61), calls=%async_computation | async-start | bytes 1048576 | tf_op jit(solution)/shard_map/all_to_all | solution.py:307
  105.1 3.3 %fusion.102 = bf16[4,256,512]{2,1,0:T(8,128)(2,1)} fusion(s32[256,512]{1,0:T(8,128)} %param.6, s32[4]{0:T(128)S(1)} %iota_add_fusion.1), kind=kLoop, calls=%fused_computation.146 | loop fusion | flops 10485760 | bytes 1572880 | tf_op jit(solution)/shard_map/neg | solution.py:315
  108.3 0.0 copy-done.2
  108.3 3.3 %add_convert_fusion = (bf16[4,256,512]{2,1,0:T(8,128)(2,1)}, bf16[4,256,512]{2,1,0:T(8,128)(2,1)}) fusion(s32[256,512]{1,0:T(8,128)S(1)} %copy-done.2, s32[4]{0:T(128)S(1)} %iota_add_fusion.1), kind=kLoop, calls=%fused_computation.38 | loop fusion | flops 15728640 | bytes 2621456 | tf_op jit(solution)/shard_map/convert_element_type | solution.py:52
  111.7 7.7 %all-to-all-done = bf16[16,2,8192]{2,1,0:T(2,128)(2,1)} async-done(((bf16[16,2,8192]{2,1,0:T(2,128)(2,1)}), bf16[16,2,8192]{2,1,0:T(2,128)(2,1)}, u32[]{:S(2)}, u32[]{:S(2)}) %all-to-all-start) | async-done | bytes 524320 | tf_op jit(solution)/shard_map/all_to_all | solution.py:307
  119.4 3.1 %reshape.62 = bf16[16,32,16,32]{3,2,1,0:T(8,128)(2,1)S(1)} reshape(bf16[16,2,8192]{2,1,0:T(2,128)(2,1)} %all-to-all-done) | data formatting | bytes 1048576
  122.4 3.6 %copy.10 = bf16[16,2,2,4,32,32]{5,0,2,4,1,3:T(8,128)(2,1)} copy(bf16[16,2,2,4,32,32]{4,3,2,1,5,0:T(4,128)(2,1)S(1)} %bitcast.24) | data formatting | bytes 1048576 | tf_op jit(solution)/shard_map/reshape | solution.py:308
  126.1 0.0 copy-start.3
  126.1 0.0 copy-start.4
  126.1 4.4 %reshape.50 = bf16[4,64,1024]{2,1,0:T(8,128)(2,1)} reshape(bf16[4,2,32,2,16,32]{5,4,3,2,1,0:T(8,128)(2,1)} %bitcast.25) | data formatting | bytes 1048576 | tf_op jit(solution)/shard_map/reshape | solution.py:309
  130.4 0.0 copy-done.3
  130.4 0.0 copy-done.4
  130.4 5.6 %fusion.8 = f32[4,64,512]{2,1,0:T(8,128)S(1)} fusion(bf16[4,64,1024]{2,1,0:T(8,128)(2,1)} %reshape.50, bf16[4,256,512]{2,1,0:T(8,128)(2,1)} %get-tuple-element.6, bf16[4,256,512]{2,1,0:T(8,128)(2,1)S(1)} %copy-done.4, bf16[4,256,512]{2,1,0:T(8,128)(2,1)S(1)} %copy-done.3), kind=kOutput, calls=%fused_computation.15 | convolution fusion | flops 285212672 | bytes 4194304 | tf_op jit(solution)/shard_map/dot_general | solution.py:320
  136.1 0.9 copy.16
  (6 shorter events, 0.1 us)
Async XLA Ops:
  0.0 2.8 %copy-start = (bf16[512,1024]{1,0:T(8,128)(2,1)S(1)}, bf16[512,1024]{1,0:T(8,128)(2,1)}, u32[]{:S(2)}) copy-start(bf16[512,1024]{1,0:T(8,128)(2,1)} %param.5) | copy-start | bytes 3145732
  5.4 2.4 %copy-start.1 = (bf16[64,38912]{1,0:T(8,128)(2,1)S(1)}, bf16[64,38912]{1,0:T(8,128)(2,1)}, u32[]{:S(2)}) copy-start(bf16[64,38912]{1,0:T(8,128)(2,1)} %voltages_ref.1) | copy-start | bytes 14942212
  92.1 16.3 %copy-start.2 = (s32[256,512]{1,0:T(8,128)S(1)}, s32[256,512]{1,0:T(8,128)}, u32[]{:S(2)}) copy-start(s32[256,512]{1,0:T(8,128)} %param.6) | copy-start | bytes 1572868
  92.1 27.3 %all-to-all-start = ((bf16[16,2,8192]{2,1,0:T(2,128)(2,1)}), bf16[16,2,8192]{2,1,0:T(2,128)(2,1)}, u32[]{:S(2)}, u32[]{:S(2)}) async-start(bf16[16,2,8192]{2,1,0:T(2,128)(2,1)} %reshape.61), calls=%async_computation | async-start | bytes 1048576 | tf_op jit(solution)/shard_map/all_to_all | solution.py:307
  126.1 4.4 %copy-start.3 = (bf16[4,256,512]{2,1,0:T(8,128)(2,1)S(1)}, bf16[4,256,512]{2,1,0:T(8,128)(2,1)}, u32[]{:S(2)}) copy-start(bf16[4,256,512]{2,1,0:T(8,128)(2,1)} %fusion.102) | copy-start | bytes 3145732
  126.1 4.4 %copy-start.4 = (bf16[4,256,512]{2,1,0:T(8,128)(2,1)S(1)}, bf16[4,256,512]{2,1,0:T(8,128)(2,1)}, u32[]{:S(2)}) copy-start(bf16[4,256,512]{2,1,0:T(8,128)(2,1)} %get-tuple-element.5) | copy-start | bytes 3145732

commit v4 on v3

--- a/solution.py
+++ b/solution.py
@@ -35,7 +35,9 @@
     turns = bin_index[:, None] * frame_index[None, :] % BLOCK_FRAMES
     angle = turns.astype(jnp.float32) * (TWO_PI / BLOCK_FRAMES)
     one = jnp.concatenate([jnp.cos(angle), -jnp.sin(angle)], 0)
-    return jnp.kron(jnp.eye(blocks, dtype=jnp.float32), one).astype(jnp.bfloat16)
+    table = jnp.kron(jnp.eye(blocks, dtype=jnp.float32), one)
+    table = table.reshape(blocks, 2, FLUCT_BINS, -1).transpose(2, 0, 1, 3)
+    return table.reshape(2 * FLUCT_BINS * blocks, -1).astype(jnp.bfloat16)
 
 
 def eighth_cos(turns):
@@ -305,23 +307,18 @@
     outgoing = fluctuation.reshape(chan_local, 2 * FLUCT_BINS * blocks, devices, beam_local)
     outgoing = outgoing.transpose(2, 1, 3, 0)
     exchanged = lax.all_to_all(outgoing, "chan", split_axis=0, concat_axis=0, tiled=True)
-    exchanged = exchanged.reshape(devices, blocks, 2, FLUCT_BINS, beam_local, chan_local)
-    parts = exchanged.transpose(3, 1, 4, 2, 0, 5).reshape(
-        FLUCT_BINS, blocks * beam_local, 2 * channels
-    )
+    parts = exchanged.reshape(devices, -1, chan_local).transpose(1, 0, 2)
+    parts = parts.reshape(FLUCT_BINS, 2 * blocks * beam_local, channels)
     trial_cos, trial_sin = trial_tables(trial_delays)
-    both = jnp.concatenate(
-        [
-            jnp.concatenate([trial_cos, -trial_sin], 2),
-            jnp.concatenate([trial_sin, trial_cos], 2),
-        ],
-        1,
-    )
+    both = jnp.concatenate([trial_cos, trial_sin], 1)
     sums = lax.dot_general(
         parts, both, (((2,), (2,)), ((0,), (0,))), preferred_element_type=jnp.float32
     )
     normaliser = 1.0 / (channels * BLOCK_FRAMES * antennas * antennas)
-    sum_real, sum_imag = sums[..., :trials], sums[..., trials:]
+    sums = sums.reshape(FLUCT_BINS, blocks, 2, beam_local, 2 * trials)
+    real, imag = sums[:, :, 0], sums[:, :, 1]
+    sum_real = real[..., :trials] - imag[..., trials:]
+    sum_imag = real[..., trials:] + imag[..., :trials]
     power = (sum_real * sum_real + sum_imag * sum_imag) * normaliser
     return power.reshape(FLUCT_BINS, blocks, beam_local, trials).transpose(1, 2, 0, 3)
 

time: 137 us -> 131 us (0.956)
  local copies, waits for them, and re-layouts: 24.1 us -> 20 us
  matrix products: 18.3 us -> 15.1 us
  waiting for transfers between devices: 7.71 us -> 9.9 us
  other arithmetic: 8.65 us -> 7.2 us
    reshape x3 -> x2, local copies, waits for them, and re-layouts: 8.88 us -> 3.92 us  [the longest x1 2.75 us: shards(): parts = exchanged.reshape(devices, -1, chan_local).transpose(1, 0, 2)]
    dot_general x1, matrix products: 5.63 us -> 2.37 us  [shards(): lax.dot_general(parts, both, (((2,), (2,)), ((0,), (0,))), preferred_elem...]
    neg x1 -> x0, other arithmetic: 3.26 us -> none  [shards(): -trial_sin]
    all_to_all x1, waiting for transfers between devices: 7.71 us -> 9.9 us  [shards(): lax.all_to_all(outgoing, 'chan', split_axis=0, concat_axis=0, tiled=True)]
    unnamed x12 -> x8, local copies, waits for them, and re-layouts: 8.13 us -> 8.82 us
  transfers between devices with their start and end apart: 1 -> 1, of which waited for: 1 -> 1; matrix products, arithmetic and copies ran while one was open for 5% -> 3% of each run, Pallas kernels for 0% -> 0%
where the time goes in v4:
time: 131 us; the launch traced here: 130 us
  Pallas kernels  64.5 us (49%)
  local copies, waits for them, and re-layouts  20 us (15%)
  matrix products  15.1 us (12%)
  starting transfers between devices  12.9 us (10%)
  waiting for transfers between devices  9.9 us (8%)
  other arithmetic  7.2 us (5%)
    pallas_call x1, Pallas kernels, form_beams(): pl.pallas_call(functools.partial(beam_kernel, channels), out_shape=jax.Sh...  61.9 us
    all_to_all x1, starting transfers between devices, shards(): lax.all_to_all(outgoing, 'chan', split_axis=0, concat_axis=0, tiled=True)  12.9 us
    dot_general x1, matrix products, shards(): lax.dot_general(filter_rows, frame_rows, (((1,), (1,)), ((), ())), prefer...  12.7 us
    all_to_all x1, waiting for transfers between devices, shards(): lax.all_to_all(outgoing, 'chan', split_axis=0, concat_axis=0, tiled=True)  9.9 us
    unnamed x8, local copies, waits for them, and re-layouts  8.82 us
    convert_element_type x1, other arithmetic, trial_tables(): cosine = eighth_cos(turns).astype(jnp.bfloat16)  4.41 us
    reshape x2, local copies, waits for them, and re-layouts, shards(): fluctuation.reshape(chan_local, 2 * FLUCT_BINS * blocks, devices, beam_lo...  4.36 us
    reshape x1, local copies, waits for them, and re-layouts, shards(): parts = exchanged.reshape(devices, -1, chan_local).transpose(1, 0, 2)  2.75 us
  transfers between devices with their start and end apart: 1, of which 1 were waited for; matrix products, arithmetic and copies ran while one was open for 3% of the time, Pallas kernels for 0%

profile of v4, /device:TPU:0, one launch (start us, length us, event | category | flops | bytes accessed | tf_op | source)
XLA Modules:
  0.0 130.4 jit_solution(2787872082596441156)
XLA Ops:
  0.0 0.0 copy-start
  0.0 0.8 fusion.84
  0.8 0.1 fusion.88
  0.9 0.1 mul.323
  1.0 0.1 mul.314
  1.1 0.1 mul.315
  1.9 0.3 fusion.58.window_ref
  2.2 0.7 compare_select_fusion.2
  2.9 0.0 copy-done
  2.9 2.1 %gather_fusion = bf16[512,1024]{1,0:T(8,128)(2,1)S(1)} fusion(bf16[512,1024]{1,0:T(8,128)(2,1)S(1)} %copy-done, s32[1024]{0:T(1024)S(1)} %pad_clamp_fusion), kind=kCustom, calls=%fused_computation | custom fusion | bytes 2099200 | tf_op jit(solution)/shard_map/gather | solution.py:304
  5.0 0.5 copy.9
  5.5 0.0 copy-start.1
  5.6 2.4 %copy-done.1 = bf16[64,38912]{1,0:T(8,128)(2,1)S(1)} copy-done((bf16[64,38912]{1,0:T(8,128)(2,1)S(1)}, bf16[64,38912]{1,0:T(8,128)(2,1)}, u32[]{:S(2)}) %copy-start.1) | copy-done | bytes 4980760
  8.0 2.6 %shard_map.46 = bf16[1024,2048]{1,0:T(8,128)(2,1)S(1)} custom-call(f32[4,2048]{1,0:T(4,128)S(1)} %fusion.58.window_ref, bf16[64,38912]{1,0:T(8,128)(2,1)S(1)} %copy-done.1), custom_call_target="tpu_custom_call" | custom-call | tf_op jit(solution)/shard_map/pallas_call | solution.py:106
  10.6 12.7 %fusion.34 = bf16[1024,1024]{1,0:T(8,128)(2,1)S(1)} fusion(bf16[1024,2048]{1,0:T(8,128)(2,1)S(1)} %shard_map.46, s32[1024]{0:T(1024)S(1)} %get-tuple-element.11, s32[1024]{0:T(1024)S(1)} %get-tuple-element.12), kind=kOutput, calls=%fused_computation.45 | convolution fusion | flops 4348444672 | bytes 6299648 | tf_op jit(solution)/shard_map/dot_general | solution.py:300
  23.3 61.9 %shard_map.47 = bf16[32,16,512]{2,1,0:T(8,128)(2,1)S(1)} custom-call(bf16[1024,512]{1,0:T(8,128)(2,1)S(1)} %bitcast.30, bf16[16,4,16,1024]{3,2,1,0:T(8,128)(2,1)S(1)} %bitcast.31, bf16[16,16]{1,0:T(8,128)(2,1)S(1)} %bitcast.32), custom_call_target="tpu_custom_call" | custom-call | tf_op jit(solution)/shard_map/pallas_call | solution.py:263
  85.2 2.2 %reshape.53 = bf16[32,16,16,32]{3,2,1,0:T(8,128)(2,1)} reshape(bf16[32,16,512]{2,1,0:T(8,128)(2,1)S(1)} %shard_map.47) | data formatting | bytes 1048576 | tf_op jit(solution)/shard_map/reshape | solution.py:307
  87.4 2.1 %copy.26 = bf16[32,16,16,32]{3,1,0,2:T(8,128)(2,1)S(1)} copy(bf16[32,16,16,32]{3,2,1,0:T(8,128)(2,1)} %reshape.53) | data formatting | bytes 1048576 | tf_op jit(solution)/shard_map/reshape | solution.py:307
  89.6 2.7 %reshape.66 = bf16[16,2,8192]{2,1,0:T(2,128)(2,1)} reshape(bf16[16,32,16,32]{3,2,1,0:T(8,128)(2,1)S(1)} %bitcast.34) | data formatting | bytes 1048576
  92.2 12.9 %all-to-all-start = ((bf16[16,2,8192]{2,1,0:T(2,128)(2,1)}), bf16[16,2,8192]{2,1,0:T(2,128)(2,1)}, u32[]{:S(2)}, u32[]{:S(2)}) async-start(bf16[16,2,8192]{2,1,0:T(2,128)(2,1)} %reshape.66), calls=%async_computation | async-start | bytes 1048576 | tf_op jit(solution)/shard_map/all_to_all | solution.py:309
  105.1 4.4 %add_convert_fusion.1 = (bf16[4,256,512]{2,1,0:T(8,128)(2,1)}, bf16[4,256,512]{2,1,0:T(8,128)(2,1)}) fusion(s32[256,512]{1,0:T(8,128)} %param.6, s32[4]{0:T(128)S(1)} %iota_add_fusion.1), kind=kLoop, calls=%fused_computation.35 | loop fusion | flops 15728640 | bytes 2621456 | tf_op jit(solution)/shard_map/convert_element_type | solution.py:53
  109.5 9.9 %all-to-all-done = bf16[16,2,8192]{2,1,0:T(2,128)(2,1)} async-done(((bf16[16,2,8192]{2,1,0:T(2,128)(2,1)}), bf16[16,2,8192]{2,1,0:T(2,128)(2,1)}, u32[]{:S(2)}, u32[]{:S(2)}) %all-to-all-start) | async-done | bytes 524320 | tf_op jit(solution)/shard_map/all_to_all | solution.py:309
  119.4 3.1 %reshape.67 = bf16[16,32,16,32]{3,2,1,0:T(8,128)(2,1)S(1)} reshape(bf16[16,2,8192]{2,1,0:T(2,128)(2,1)} %all-to-all-done) | data formatting | bytes 1048576
  122.5 2.8 %reshape.54 = bf16[16,512,32]{1,2,0:T(8,128)(2,1)} reshape(bf16[16,16,32,32]{2,1,3,0:T(8,128)(2,1)S(1)} %bitcast.33) | data formatting | bytes 1048576 | tf_op jit(solution)/shard_map/reshape | solution.py:310
  125.2 1.2 reshape.55
  126.4 2.4 %fusion.22 = f32[4,128,512]{2,1,0:T(8,128)S(1)} fusion(bf16[4,256,512]{2,1,0:T(8,128)(2,1)} %get-tuple-element.8, bf16[4,256,512]{2,1,0:T(8,128)(2,1)} %get-tuple-element.7, bf16[4,128,512]{1,0,2:T(4,128)(2,1)S(1)} %reshape.55), kind=kOutput, calls=%fused_computation.29 | convolution fusion | flops 272629760 | bytes 3670016 | tf_op jit(solution)/shard_map/dot_general | solution.py:314
  128.8 0.1 fusion.102
  128.8 0.3 copy.24
  129.2 0.3 copy.25
  129.5 0.8 fusion.41
  (8 shorter events, 0.0 us)
Async XLA Ops:
  0.0 2.9 %copy-start = (bf16[512,1024]{1,0:T(8,128)(2,1)S(1)}, bf16[512,1024]{1,0:T(8,128)(2,1)}, u32[]{:S(2)}) copy-start(bf16[512,1024]{1,0:T(8,128)(2,1)} %param.5) | copy-start | bytes 3145732
  5.5 2.4 %copy-start.1 = (bf16[64,38912]{1,0:T(8,128)(2,1)S(1)}, bf16[64,38912]{1,0:T(8,128)(2,1)}, u32[]{:S(2)}) copy-start(bf16[64,38912]{1,0:T(8,128)(2,1)} %voltages_ref.1) | copy-start | bytes 14942212
  92.2 27.2 %all-to-all-start = ((bf16[16,2,8192]{2,1,0:T(2,128)(2,1)}), bf16[16,2,8192]{2,1,0:T(2,128)(2,1)}, u32[]{:S(2)}, u32[]{:S(2)}) async-start(bf16[16,2,8192]{2,1,0:T(2,128)(2,1)} %reshape.66), calls=%async_computation | async-start | bytes 1048576 | tf_op jit(solution)/shard_map/all_to_all | solution.py:309
